TPU v7x, 768 devices: a whole 4x8x12 slice. The times are simulated.
768 devices in a mesh: dp: 64 (over x, y, core), seq: 12 (over z).
Axes of the slice: x: 4, y: 8, z: 12, core: 2. Of those that a mesh axis runs over, the one named last changes fastest.
Arguments:
- audio_blocks: bfloat16 [64, 1536, 40], P('dp', 'seq'), may hold values from -6 to 6
- send_list: int32 [12, 64, 256], P('seq', 'dp'), may hold values from -1 to 127, as said below
- place_list: int32 [12, 64, 128], P('seq', 'dp'), may hold values from 0 to 255, as said below
- cotangent: bfloat16 [64, 6144, 512], P('dp', 'seq'), may hold values from -0.009765625 to 0.009765625
- conv_zero: bfloat16 [10, 512], replicated, may hold values from -2 to 2
- conv_one: bfloat16 [1536, 512], replicated, may hold values from -0.15625 to 0.15625
- gain_zero: float32 [512], replicated, may hold values from 0.25 to 1.75
- bias_zero: float32 [512], replicated, may hold values from -3 to 3
- gain_one: float32 [512], replicated, may hold values from 0.25 to 1.75
- bias_one: float32 [512], replicated, may hold values from -3 to 3
Outputs:
- features: bfloat16 [64, 6144, 512], P('dp', 'seq')
- grad_conv_one: float32 [1536, 512], P('dp')
- grad_conv_zero: float32 [10, 512], replicated
- grad_gain_zero: float32 [512], replicated
- grad_bias_zero: float32 [512], replicated
- grad_gain_one: float32 [512], replicated
- grad_bias_one: float32 [512], replicated
Inputs may be any that keep to these rules, and one draw needn't show every extreme that they name: `send_list`: row (s, i) holds, in 4 slots for each destination device in order, the local blocks of store s on device i sent there; -1 marks an empty slot. Each of the 128 blocks appears exactly once in its row, and in every store some source fills all 4 slots to some destination. `place_list`: row (s, j) names 128 distinct filled received slots (source times 4 plus slot) for device j and store s, in the order of its segment.
All inputs are finite; a program needn't handle non-finite values.
Results may differ from a plain program's by a relative error of at most 0.0057.
Values may be sent and summed in bfloat16 or wider, within the bound.
A program may use at most 64 MiB of HBM per device.

v0:
```python
import jax
import jax.numpy as jnp
from jax import lax
from jax.sharding import PartitionSpec as P

norm_eps = 1e-05


def shifted(block, axis, distance):
    devices = range(lax.axis_size(axis))
    route = [(i - distance, i) for i in devices if i - distance in devices]
    return lax.ppermute(block, axis, route)


def in_blocks(array, dim, count):
    shape = array.shape
    parts = array.reshape(*shape[:dim], count, shape[dim] // count, *shape[dim + 1 :])
    return jnp.moveaxis(parts, dim, 0)


def sent_and_summed(array, axis, dim):
    count = lax.axis_size(axis)
    parts = lax.all_to_all(in_blocks(array, dim, count), axis, 0, 0, tiled=True)
    return jnp.sum(parts, axis=0)


def from_everyone(array, axis):
    count = lax.axis_size(axis)
    return lax.all_to_all(
        jnp.broadcast_to(array[None], (count, *array.shape)), axis, 0, 0, tiled=True
    )


def of_everyone(array, axis):
    everything = from_everyone(array, axis)
    return jnp.sum(everything, axis=0)


def gelu_slope(argument):
    return (
        0.5 * (1.0 + lax.erf(argument * 0.7071067811865476))
        + argument * jnp.exp(-0.5 * argument * argument) * 0.3989422804014327
    )


def norm_forward(pre_act, gain_vec, bias_vec):
    center = pre_act - jnp.mean(pre_act, axis=-1, keepdims=True)
    spread = lax.rsqrt(jnp.mean(center * center, axis=-1, keepdims=True) + norm_eps)
    scaled = center * spread
    normed = scaled * gain_vec + bias_vec
    return (jax.nn.gelu(normed, approximate=False), scaled, spread, normed)


def norm_backward(upstream, gain_vec, scaled, spread, normed):
    inner_grad = upstream * gelu_slope(normed)
    grad_gain = jnp.sum(inner_grad * scaled, axis=0)
    grad_bias = jnp.sum(inner_grad, axis=0)
    pushed = inner_grad * gain_vec
    back_grad = spread * (
        pushed
        - jnp.mean(pushed, axis=-1, keepdims=True)
        - scaled * jnp.mean(pushed * scaled, axis=-1, keepdims=True)
    )
    return (back_grad, grad_gain, grad_bias)


def frame_patches(samples, frames):
    sample_rows = samples.reshape(frames + 1, 5)
    return jnp.concatenate([sample_rows[:-1], sample_rows[1:]], axis=1)


def layer_one(frames_in, frames_one, conv_one, gain_one, bias_one, upstream):
    width = conv_one.shape[1]
    frame_pairs = frames_in[: 2 * frames_one].reshape(frames_one, 2, width)
    first_tap = frame_pairs[:, 0]
    second_tap = frame_pairs[:, 1]
    third_tap = jnp.concatenate([first_tap[1:], frames_in[2 * frames_one :]], axis=0)
    pre_one = (
        jnp.dot(first_tap, conv_one[:width], preferred_element_type=jnp.float32)
        + jnp.dot(second_tap, conv_one[width : 2 * width], preferred_element_type=jnp.float32)
        + jnp.dot(third_tap, conv_one[2 * width :], preferred_element_type=jnp.float32)
    )
    act_one, scaled_one, spread_one, normed_one = norm_forward(pre_one, gain_one, bias_one)
    back_one, grad_gain_one, grad_bias_one = norm_backward(
        upstream.astype(jnp.float32), gain_one, scaled_one, spread_one, normed_one
    )
    back_one = back_one.astype(jnp.bfloat16)
    grad_conv_one = jnp.concatenate(
        [
            jnp.dot(first_tap.T, back_one, preferred_element_type=jnp.float32),
            jnp.dot(second_tap.T, back_one, preferred_element_type=jnp.float32),
            jnp.dot(third_tap.T, back_one, preferred_element_type=jnp.float32),
        ],
        axis=0,
    )
    to_first = jnp.dot(back_one, conv_one[:width].T, preferred_element_type=jnp.float32)
    to_second = jnp.dot(back_one, conv_one[width : 2 * width].T, preferred_element_type=jnp.float32)
    to_third = jnp.dot(back_one, conv_one[2 * width :].T, preferred_element_type=jnp.float32)
    even_grad = to_first + jnp.concatenate(
        [jnp.zeros((1, width), jnp.float32), to_third[:-1]], axis=0
    )
    frame_grad = jnp.stack([even_grad, to_second], axis=1).reshape(2 * frames_one, width)
    return (
        act_one.astype(jnp.bfloat16),
        grad_conv_one,
        grad_gain_one,
        grad_bias_one,
        frame_grad,
        to_third[-1:],
    )


def attach_rows(pieces, extra_rows):
    copies = jnp.broadcast_to(extra_rows[None], (pieces.shape[0],) + extra_rows.shape)
    return jnp.concatenate([pieces, copies], axis=1).reshape(-1, pieces.shape[2])


def on_device(
    audio_blocks,
    send_list,
    place_list,
    cotangent,
    conv_zero,
    conv_one,
    gain_zero,
    bias_zero,
    gain_one,
    bias_one,
):
    n_data = lax.axis_size("dp")
    n_time = lax.axis_size("seq")
    width = conv_one.shape[1]
    blocks = audio_blocks[0]
    sends = send_list[0, 0]
    slot_count = sends.shape[0] // n_data
    picked = jnp.take(blocks, jnp.clip(sends, 0, blocks.shape[0] - 1), axis=0)
    picked = jnp.where((sends >= 0)[:, None], picked, jnp.zeros_like(picked))
    outgoing = picked.reshape(n_data, slot_count * blocks.shape[1])
    incoming = lax.all_to_all(outgoing, "dp", split_axis=0, concat_axis=0, tiled=True)
    arrived = incoming.reshape(n_data * slot_count, blocks.shape[1])
    samples = jnp.take(arrived, place_list[0, 0], axis=0).reshape(-1)
    next_rim = shifted(samples[:10], "seq", -1)
    extended = jnp.concatenate([samples, next_rim])
    frames_zero = samples.shape[0] // 5
    patches = frame_patches(extended, frames_zero + 1)
    pre_zero = jnp.dot(patches, conv_zero, preferred_element_type=jnp.float32)
    act_zero, scaled_zero, spread_zero, normed_zero = norm_forward(pre_zero, gain_zero, bias_zero)
    keep_flag = (lax.axis_index("seq") < n_time - 1).astype(jnp.float32)
    frames_in = act_zero.astype(jnp.bfloat16)
    frames_in = jnp.concatenate(
        [frames_in[:frames_zero], frames_in[frames_zero:] * keep_flag.astype(jnp.bfloat16)], axis=0
    )
    feats, grad_one, gain_one_grad, bias_one_grad, frame_grad, tail_grad = layer_one(
        frames_in, frames_zero // 2, conv_one, gain_one, bias_one, cotangent[0]
    )
    full_grad = jnp.concatenate([frame_grad, tail_grad * keep_flag], axis=0)
    back_zero, gain_zero_grad, bias_zero_grad = norm_backward(
        full_grad, gain_zero, scaled_zero, spread_zero, normed_zero
    )
    grad_zero = jnp.dot(patches.astype(jnp.float32).T, back_zero, precision=lax.Precision.HIGHEST)
    small_rows = jnp.concatenate(
        [
            grad_zero,
            jnp.stack([gain_zero_grad, bias_zero_grad, gain_one_grad, bias_one_grad], axis=0),
        ],
        axis=0,
    )
    rows_part = grad_one.shape[0] // n_data
    packed = attach_rows(grad_one.reshape(n_data, rows_part, width), small_rows)
    data_share = sent_and_summed(packed, "dp", 0)
    combined = of_everyone(data_share, "seq")
    grad_rows = combined[:rows_part]
    small_total = combined[rows_part:]
    small_count = small_rows.shape[0]
    grad_zero_sum = small_total[: small_count - 4]
    gain_zero_sum = small_total[small_count - 4]
    bias_zero_sum = small_total[small_count - 3]
    gain_one_sum = small_total[small_count - 2]
    bias_one_sum = small_total[small_count - 1]
    return (
        feats[None],
        grad_rows,
        grad_zero_sum,
        gain_zero_sum,
        bias_zero_sum,
        gain_one_sum,
        bias_one_sum,
    )


def solution(mesh):
    placed = (
        P("dp", "seq", None),
        P("seq", "dp", None),
        P("seq", "dp", None),
        P("dp", "seq", None),
        P(),
        P(),
        P(),
        P(),
        P(),
        P(),
    )
    return jax.shard_map(
        on_device,
        mesh=mesh,
        in_specs=placed,
        out_specs=(P("dp", "seq", None), P("dp", None), P(), P(), P(), P(), P()),
        check_vma=False,
    )
```

profile of v0, /device:TPU:1, one launch (start us, length us, event | category | flops | bytes accessed | tf_op | source)
XLA Modules:
  0.0 259.9 jit_solution(11404842790577545637)
XLA Ops:
  0.6 0.7 compare_reduce_fusion
  1.4 0.7 compare_select_fusion.1
  2.0 0.7 clamp_reduce_fusion
  2.7 0.1 ge.39
  2.9 0.1 min.16
  3.2 0.8 copy.47
  4.0 0.9 gather_fusion
  4.9 0.1 gather.11
  5.0 0.1 copy.48
  5.1 0.7 copy.49
  5.9 14.6 %all-to-all-start = ((bf16[64,1,160]{2,1,0:T(2,128)(2,1)}), bf16[64,1,160]{2,1,0:T(2,128)(2,1)S(1)}, u32[]{:S(2)}, u32[]{:S(2)}) async-start(bf16[64,1,160]{2,1,0:T(2,128)(2,1)} %copy.49), calls=%async_computation | async-start | bytes 131072 | tf_op jit(solution)/shard_map/all_to_all | solution.py:139
  20.4 0.7 fusion.55
  21.1 0.7 compare_and_fusion.1
  21.8 2.0 copy.55
  23.8 6.5 %all-to-all-done = bf16[64,1,160]{2,1,0:T(2,128)(2,1)S(1)} async-done(((bf16[64,1,160]{2,1,0:T(2,128)(2,1)}), bf16[64,1,160]{2,1,0:T(2,128)(2,1)S(1)}, u32[]{:S(2)}, u32[]{:S(2)}) %all-to-all-start) | async-done | bytes 20512 | tf_op jit(solution)/shard_map/all_to_all | solution.py:139
  30.3 0.2 reduce.2
  30.6 0.7 gather_fusion.1
  31.4 0.1 select_n.72
  31.6 1.3 collective-permute-start
  32.9 3.0 %collective-permute-done = bf16[10]{0:T(256)(128)(2,1)S(1)} collective-permute-done((bf16[10]{0:T(256)(128)(2,1)S(1)}, bf16[10]{0:T(256)(128)(2,1)S(1)}, u32[]{:S(2)}, u32[]{:S(2)}) %collective-permute-start) | collective-permute-done | bytes 52 | tf_op jit(solution)/shard_map/ppermute | solution.py:12
  35.9 0.4 slice.94
  36.4 0.2 copy.50
  36.5 0.4 slice.96
  37.0 0.2 copy.51
  37.1 0.6 fusion.65
  37.7 0.4 multiply_reduce_fusion.2
  38.2 5.8 %fusion.2 = bf16[1025,512]{1,0:T(8,128)(2,1)S(1)} fusion(f32[1025,512]{1,0:T(8,128)S(1)} %get-tuple-element.55, f32[512]{0:T(512)S(1)} %copy-done.8, f32[512]{0:T(512)S(1)} %copy-done.7, f32[1025]{0:T(1024)S(1)} %add_rsqrt_fusion, f32[1025]{0:T(1024)S(1)} %broadcast_multiply_fusion.2), kind=kLoop, calls=%fused_computation.8 | loop fusion | flops 36211200 | bytes 3161096 | tf_op jit(solution)/shard_map/convert_element_type | solution.py:149
  44.0 1.0 copy-done.2
  45.0 1.1 slice.121
  46.1 1.5 reshape.210
  47.5 0.7 slice.124
  48.3 1.5 fusion.62
  49.8 0.7 slice_multiply_fusion.1
  50.5 0.1 copy.68
  50.6 0.5 fusion.49
  51.1 0.5 convolution_add_fusion.2
  51.7 0.5 fusion.66
  52.2 0.2 multiply_reduce_fusion.6
  52.4 0.3 copy-done.5
  52.7 4.2 %multiply_reduce_fusion.4 = (f32[512]{0:T(512)S(1)}, f32[512]{0:T(512)S(1)}, f32[512]{0:T(512)S(1)}, f32[512]{0:T(512)S(1)}, f32[512,512]{0,1:T(8,128)S(1)}, /*index=5*/bf16[1,512,512]{1,2,0:T(8,128)(2,1)}) fusion(f32[512,512]{0,1:T(8,128)S(1)} %get-tuple-element.57, f32[512]{0:T(512)S(1)} %add_rsqrt_fusion.1, f32[512]{0:T(512)S(1)} %broadcast_multiply_fusion.5, ...), kind=kLoop, calls=%fused_computation.62 | loop fusion | flops 22542336 | bytes 3162112 | tf_op jit(solution)/shard_map/reduce_sum | solution.py:56
  56.9 0.3 multiply_convert_fusion
  57.2 1.5 fusion.53
  58.7 1.5 fusion.52
  60.2 0.5 fusion.51
  60.7 0.5 fusion.43
  61.2 0.5 convolution_bitcast_fusion
  61.7 0.5 fusion.21
  62.2 0.2 pad_maximum_fusion.2
  62.3 3.0 %copy.56 = f32[512,2,512]{2,1,0:T(2,128)} copy(f32[512,2,512]{2,0,1:T(8,128)S(1)} %pad_maximum_fusion.2) | data formatting | bytes 4194304 | tf_op jit(solution)/shard_map/stack | solution.py:102
  65.3 3.7 %reshape.212 = f32[1024,512]{1,0:T(8,128)} reshape(f32[512,2,512]{2,1,0:T(2,128)} %copy.56) | data formatting | bytes 4194304 | tf_op jit(solution)/shard_map/reshape | solution.py:102
  69.0 3.8 %multiply_reduce_fusion = (f32[512]{0:T(512)S(1)}, f32[1025]{0:T(1024)S(1)}, f32[1025]{0:T(1024)S(1)}, f32[512]{0:T(512)S(1)}, f32[1025,512]{1,0:T(8,128)S(1)}) fusion(f32[1025,512]{1,0:T(8,128)S(1)} %get-tuple-element.55, f32[1025]{0:T(1024)S(1)} %add_rsqrt_fusion, f32[1025]{0:T(1024)S(1)} %broadcast_multiply_fusion.2, f32[512]{0:T(512)S(1)} %copy-done.7, ...), kind=kLoop, calls=%fused_computation.14 | loop fusion | flops 11017726 | bytes 6322192 | tf_op jit(solution)/shard_map/reduce_sum | solution.py:56
  72.8 2.0 pad_maximum_fusion.1
  74.8 1.4 fusion.8
  76.2 0.3 broadcast_in_dim.75
  76.5 2.7 %pad_maximum_fusion = f32[64,38,512]{2,1,0:T(8,128)S(1)} fusion(f32[64,14,512]{2,1,0:T(8,128)S(1)} %broadcast_in_dim.75, f32[64,24,512]{2,1,0:T(8,128)} %bitcast.56), kind=kLoop, calls=%fused_computation.2 | loop fusion | flops 1245184 | bytes 9961472 | tf_op jit(solution)/shard_map/concatenate | solution.py:115
  79.1 124.0 %all_to_all.16 = f32[64,38,512]{2,1,0:T(8,128)} all-to-all(f32[64,38,512]{2,1,0:T(8,128)S(1)} %pad_maximum_fusion), channel_id=1, replica_groups=mesh['dp'=64,'seq'=12] {'dp'}, dimensions={0} | all-to-all | bytes 9961472 | tf_op jit(solution)/shard_map/all_to_all | solution.py:23
  203.1 2.9 %reduce_sum.138 = f32[38,512]{1,0:T(8,128)S(1)} reduce(f32[64,38,512]{2,1,0:T(8,128)} %all_to_all.16, f32[]{:T(128)} %constant.50.clone.1), dimensions={0}, to_apply=%region_12.13 | reduce | flops 1225728 | bytes 5058564 | tf_op jit(solution)/shard_map/reduce_sum | solution.py:24
  206.0 1.1 broadcast_in_dim.76
  207.1 13.1 %all-to-all-start.2 = ((f32[12,38,512]{2,1,0:T(8,128)}), f32[12,38,512]{2,1,0:T(8,128)S(1)}, u32[]{:S(2)}, u32[]{:S(2)}) async-start(f32[12,38,512]{2,1,0:T(8,128)} %broadcast_in_dim.76), calls=%async_computation.2 | async-start | bytes 1966080 | tf_op jit(solution)/shard_map/all_to_all | solution.py:29
  220.2 1.0 copy.57
  221.2 36.8 %all-to-all-done.2 = f32[12,38,512]{2,1,0:T(8,128)S(1)} async-done(((f32[12,38,512]{2,1,0:T(8,128)}), f32[12,38,512]{2,1,0:T(8,128)S(1)}, u32[]{:S(2)}, u32[]{:S(2)}) %all-to-all-start.2) | async-done | bytes 933920 | tf_op jit(solution)/shard_map/all_to_all | solution.py:29
  258.0 0.6 fusion.63
  258.6 0.6 slice.129
  259.2 0.6 slice.128
  (44 shorter events, 0.7 us)
Async XLA Ops:
  0.6 36.5 %copy-start = (bf16[10,512]{1,0:T(8,128)(2,1)S(1)}, bf16[10,512]{1,0:T(8,128)(2,1)}, u32[]{:S(2)}) copy-start(bf16[10,512]{1,0:T(8,128)(2,1)} %param.14) | copy-start | bytes 30724
  5.9 24.5 %all-to-all-start = ((bf16[64,1,160]{2,1,0:T(2,128)(2,1)}), bf16[64,1,160]{2,1,0:T(2,128)(2,1)S(1)}, u32[]{:S(2)}, u32[]{:S(2)}) async-start(bf16[64,1,160]{2,1,0:T(2,128)(2,1)} %copy.49), calls=%async_computation | async-start | bytes 131072 | tf_op jit(solution)/shard_map/all_to_all | solution.py:139
  31.6 4.3 %collective-permute-start = (bf16[10]{0:T(256)(128)(2,1)S(1)}, bf16[10]{0:T(256)(128)(2,1)S(1)}, u32[]{:S(2)}, u32[]{:S(2)}) collective-permute-start(bf16[10]{0:T(256)(128)(2,1)S(1)} %slice.118), channel_id=1, source_target_pairs={{1,0},{2,1},{3,2},{4,3},{5,4},{6,5},{7,6},{8,7},{9,8},{10,9},{11,1... | collective-permute-start | bytes 68 | tf_op jit(solution)/shard_map/ppermute | solution.py:12
  37.1 1.1 copy-start.7
  37.1 1.1 copy-start.8
  44.0 1.0 copy-start.2
  48.3 2.4 copy-start.1
  51.6 1.0 copy-start.5
  51.6 1.0 copy-start.9
  51.6 1.0 copy-start.10
  69.0 3.8 %copy-start.3 = (f32[512,512]{1,0:T(8,128)S(1)}, f32[512,512]{1,0:T(8,128)}, u32[]{:S(2)}) copy-start(f32[512,512]{1,0:T(8,128)} %fusion.53) | copy-start | bytes 3145732
  69.0 3.8 %copy-start.4 = (f32[512,512]{1,0:T(8,128)S(1)}, f32[512,512]{1,0:T(8,128)}, u32[]{:S(2)}) copy-start(f32[512,512]{1,0:T(8,128)} %fusion.52) | copy-start | bytes 3145732
  206.0 14.2 %copy-start.6 = (bf16[1,512,512]{1,2,0:T(8,128)(2,1)S(1)}, bf16[1,512,512]{1,2,0:T(8,128)(2,1)}, u32[]{:S(2)}) copy-start(bf16[1,512,512]{1,2,0:T(8,128)(2,1)} %get-tuple-element.45) | copy-start | bytes 1572868
  207.1 50.9 %all-to-all-start.2 = ((f32[12,38,512]{2,1,0:T(8,128)}), f32[12,38,512]{2,1,0:T(8,128)S(1)}, u32[]{:S(2)}, u32[]{:S(2)}) async-start(f32[12,38,512]{2,1,0:T(8,128)} %broadcast_in_dim.76), calls=%async_computation.2 | async-start | bytes 1966080 | tf_op jit(solution)/shard_map/all_to_all | solution.py:29
where the time goes:
time: 261 us; the launch traced here: 260 us
  blocking collectives  124 us (48%)
  waiting for transfers between devices  46.3 us (18%)
  starting transfers between devices  28.9 us (11%)
  other arithmetic  27 us (10%)
  local copies, waits for them, and re-layouts  24.3 us (9%)
  matrix products  8.34 us (3%)
    all_to_all x1, blocking collectives, sent_and_summed(): parts = lax.all_to_all(in_blocks(array, dim, count), axis, 0, 0, tiled=True)  124 us
    all_to_all x1, waiting for transfers between devices, from_everyone(): lax.all_to_all(jnp.broadcast_to(array[None], (count, *array.shape)), axis...  36.8 us
    all_to_all x1, starting transfers between devices, on_device(): lax.all_to_all(outgoing, 'dp', split_axis=0, concat_axis=0, tiled=True)  14.6 us
    all_to_all x1, starting transfers between devices, from_everyone(): lax.all_to_all(jnp.broadcast_to(array[None], (count, *array.shape)), axis...  13.1 us
    reduce_sum x2, other arithmetic, norm_backward(): grad_gain = jnp.sum(inner_grad * scaled, axis=0)  8.02 us
    all_to_all x1, waiting for transfers between devices, on_device(): lax.all_to_all(outgoing, 'dp', split_axis=0, concat_axis=0, tiled=True)  6.5 us
    convert_element_type x1, other arithmetic, on_device(): frames_in = act_zero.astype(jnp.bfloat16)  5.77 us
    unnamed x27, local copies, waits for them, and re-layouts  5.34 us
  transfers between devices with their start and end apart: 3, of which 3 were waited for; matrix products, arithmetic and copies ran while one was open for 2% of the time, Pallas kernels for 0%

commit v1 on v0

v1 whole, which is shorter than its diff:
```python
import functools

import jax
import jax.numpy as jnp
from jax import lax
from jax.experimental import pallas as pl
from jax.experimental.pallas import tpu as pltpu
from jax.sharding import PartitionSpec as P

MESH = pl.DeviceIdType.MESH
F32 = jnp.float32
BF16 = jnp.bfloat16
norm_eps = 1e-05
n_core = 2
n_y = 8
slots = 4
group = 64
lanes = slots * group
chunk_rows = 64
tail_rows = 16


def iota(shape, dim):
    return lax.broadcasted_iota(jnp.int32, shape, dim)


def one_hot(mask):
    return jnp.where(mask, 1.0, 0.0).astype(BF16)


def dot(a, b, dims=((1,), (0,))):
    return lax.dot_general(a, b, (dims, ((), ())), preferred_element_type=F32)


TN = ((0,), (0,))
NT = ((1,), (1,))


def norm_gelu(pre, gain, bias):
    center = pre - jnp.mean(pre, axis=-1, keepdims=True)
    spread = lax.rsqrt(jnp.mean(center * center, axis=-1, keepdims=True) + norm_eps)
    scaled = center * spread
    normed = scaled * gain + bias
    below = 0.5 + 0.5 * lax.erf(normed * 0.7071067811865476)
    act = normed * below
    slope = below + normed * (jnp.exp(-0.5 * normed * normed) * 0.3989422804014327)
    return act, scaled, spread, slope


def norm_back(upstream, gain, scaled, spread, slope):
    inner = upstream * slope
    pushed = inner * gain
    back = spread * (
        pushed
        - jnp.mean(pushed, axis=-1, keepdims=True)
        - scaled * jnp.mean(pushed * scaled, axis=-1, keepdims=True)
    )
    return back, inner * scaled, inner


def fold_rows(array):
    return jnp.sum(array.reshape(array.shape[0] // 8, 8, array.shape[1]), axis=0)


def kernel(
    sizes,
    audio_ref,
    send_ref,
    place_ref,
    cot_ref,
    wz_ref,
    w_ref,
    gz_ref,
    bz_ref,
    g1_ref,
    b1_ref,
    feats_ref,
    grad_ref,
    gwz_ref,
    ggz_ref,
    gbz_ref,
    gg1_ref,
    gb1_ref,
    msg,
    arr,
    own_row,
    rim,
    samples,
    patches,
    wz_pad,
    act_even,
    act_odd,
    scaled_even,
    scaled_odd,
    slope_even,
    slope_odd,
    spread_even,
    spread_odd,
    third,
    back_one,
    back_f32,
    back_down,
    hi_even,
    lo_even,
    hi_odd,
    lo_odd,
    parts,
    got_core,
    sum_core,
    got_x,
    sum_x,
    got_y,
    sum_y,
    got_z,
    small,
    small_core,
    small_x,
    small_y,
    small_z,
    small_half,
    small_full,
    msg_send,
    msg_recv,
    rim_sems,
    core_sems,
    x_send,
    x_recv,
    y_send,
    y_recv,
    z_send,
    z_recv,
    sc_sems,
    sx_send,
    sx_recv,
    sy_send,
    sy_recv,
    sz_send,
    sz_recv,
    sf_sems,
):
    n_dp, n_x, n_z, n_rows, n_out, width = sizes
    n_even = n_out + tail_rows
    me = lax.axis_index("dp")
    z = lax.axis_index("seq")
    core = lax.rem(me, n_core)
    y = lax.rem(me // n_core, n_y)
    x = me // (n_core * n_y)

    def dp_of(px, py, pc):
        return (px * n_y + py) * n_core + pc

    barrier = pltpu.get_barrier_semaphore()

    def greet_dp(k, carry):
        pl.semaphore_signal(
            barrier, inc=1, device_id={"dp": lax.rem(me + k, n_dp)}, device_id_type=MESH
        )
        return carry

    def greet_z(k, carry):
        pl.semaphore_signal(
            barrier, inc=1, device_id={"seq": lax.rem(z + k, n_z)}, device_id_type=MESH
        )
        return carry

    lax.fori_loop(1, n_dp, greet_dp, 0)
    lax.fori_loop(1, n_z, greet_z, 0)

    spread_lanes = one_hot(
        jnp.bitwise_and(iota((40, lanes), 1), group - 1) == iota((40, lanes), 0)
    )
    blocks = dot(audio_ref[...], spread_lanes, TN).astype(BF16)
    chosen = one_hot(iota((n_rows, n_dp * slots), 0) == send_ref[...])
    picked = dot(chosen, blocks, TN)
    slot_of = jnp.bitwise_and(iota((n_dp * slots, lanes), 0), slots - 1)
    lane_group = lax.shift_right_logical(iota((n_dp * slots, lanes), 1), 6)
    in_group = slot_of == lane_group
    picked = jnp.where(in_group, picked, 0.0).astype(BF16)
    gather_dest = one_hot(
        lax.shift_right_logical(iota((n_dp, n_dp * slots), 1), 2) == iota((n_dp, n_dp * slots), 0)
    )
    message = dot(gather_dest, picked)
    for d in range(n_dp):
        msg[d] = message[d : d + 1]

    pl.semaphore_wait(barrier, n_dp - 1 + n_z - 1)

    def msg_copy(k):
        peer = lax.rem(me + k, n_dp)
        return pltpu.make_async_remote_copy(
            src_ref=msg.at[peer],
            dst_ref=arr.at[me],
            send_sem=msg_send.at[k],
            recv_sem=msg_recv.at[k],
            device_id={"dp": peer},
            device_id_type=MESH,
        )

    def start_msg(k, carry):
        msg_copy(k).start()
        return carry

    lax.fori_loop(1, n_dp, start_msg, 0)
    arr[me] = msg[me]

    wz_pad[...] = jnp.zeros_like(wz_pad)
    wz_pad[0:10, :] = wz_ref[...]
    gain_zero, bias_zero = gz_ref[...], bz_ref[...]
    gain_one, bias_one = g1_ref[...], b1_ref[...]
    keep = jnp.where(z < n_z - 1, 1.0, 0.0).astype(F32)
    placed = one_hot(iota((n_dp * slots, n_rows), 0) == place_ref[...])
    spread_slots = one_hot(
        lax.shift_right_logical(iota((n_dp * slots, n_dp), 0), 2) == iota((n_dp * slots, n_dp), 1)
    )
    lane_in, lane_out = iota((lanes, lanes), 0), iota((lanes, lanes), 1)
    sample_in = jnp.bitwise_and(lane_in, group - 1)
    sample_out = jnp.bitwise_and(lane_out, group - 1)
    fold_here = one_hot((sample_in == sample_out) & (sample_out < 40))
    fold_next = one_hot((sample_in + 40 == sample_out) & (sample_out < 45))
    row_id = iota((n_even, n_rows + 8), 0)
    widen = one_hot(lax.shift_right_logical(row_id, 2) == iota((n_even, n_rows + 8), 1))
    phase = jnp.bitwise_and(iota((n_even, lanes), 0), 3)
    own_phase = phase == lax.shift_right_logical(iota((n_even, lanes), 1), 6)
    tap = sample_in - 10 * lax.shift_right_logical(lane_in, 6)
    wanted = jnp.where(lane_out < 128, lane_out, lane_out - 128 + 5)
    limit = jnp.where(lane_out < 128, 10, 15)
    to_patch = one_hot((tap == wanted) & (wanted < limit))

    def wait_msg(k, carry):
        msg_copy(k).wait_recv()
        return carry

    lax.fori_loop(1, n_dp, wait_msg, 0)

    received = jnp.concatenate([arr[s] for s in range(n_dp)], axis=0).astype(BF16)
    by_slot = dot(spread_slots, received)
    by_slot = jnp.where(in_group, by_slot, 0.0).astype(BF16)
    ordered = dot(placed, by_slot, TN)
    own_row[...] = ordered[0:8]
    rim_copy = pltpu.make_async_remote_copy(
        src_ref=own_row,
        dst_ref=rim,
        send_sem=rim_sems.at[0],
        recv_sem=rim_sems.at[1],
        device_id={"seq": lax.rem(z + n_z - 1, n_z)},
        device_id_type=MESH,
    )
    rim_copy.start()
    samples[0:n_rows, :] = ordered
    samples[n_rows : n_rows + 16, :] = jnp.zeros((16, lanes), F32)
    rim_copy.wait_recv()
    rim_lane = jnp.bitwise_and(iota((8, lanes), 1), group - 1)
    rim_row = iota((8, lanes), 0)
    samples[n_rows : n_rows + 8, :] = jnp.where(
        (rim_row == 0) & (rim_lane < 10), rim[...] * keep, 0.0
    )

    wide = dot(samples[0 : n_rows + 8, :].astype(BF16), fold_here) + dot(
        samples[1 : n_rows + 9, :].astype(BF16), fold_next
    )
    rows = dot(widen, wide.astype(BF16))
    rows = jnp.where(own_phase, rows, 0.0).astype(BF16)
    patches[...] = dot(rows, to_patch).astype(BF16)

    def forward_even(r, n):
        pre = dot(patches[pl.ds(r, n), 0:128], wz_pad[...])
        act, scaled, spread, slope = norm_gelu(pre, gain_zero, bias_zero)
        scaled_even[pl.ds(r, n), :] = scaled
        slope_even[pl.ds(r, n), :] = slope
        spread_even[pl.ds(r, n), :] = spread
        return act

    def forward_zero(i, carry):
        r = pl.multiple_of(i * chunk_rows, chunk_rows)
        act_even[pl.ds(r, chunk_rows), :] = forward_even(r, chunk_rows).astype(BF16)
        pre = dot(patches[pl.ds(r, chunk_rows), 128:256], wz_pad[...])
        act, scaled, spread, slope = norm_gelu(pre, gain_zero, bias_zero)
        act_odd[pl.ds(r, chunk_rows), :] = act.astype(BF16)
        scaled_odd[pl.ds(r, chunk_rows), :] = scaled
        slope_odd[pl.ds(r, chunk_rows), :] = slope
        spread_odd[pl.ds(r, chunk_rows), :] = spread
        return carry

    lax.fori_loop(0, n_out // chunk_rows, forward_zero, 0)
    act_even[n_out:n_even, :] = (forward_even(n_out, tail_rows) * keep).astype(BF16)

    third[...] = dot(act_even[...], w_ref[2 * width : 3 * width, :])
    third[0:n_out, :] = third[1 : n_out + 1, :]

    def layer_one(i, carry):
        sum_gain, sum_bias = carry
        r = pl.multiple_of(i * chunk_rows, chunk_rows)
        here = pl.ds(r, chunk_rows)
        pre = (
            dot(act_even[here, :], w_ref[0:width, :])
            + dot(act_odd[here, :], w_ref[width : 2 * width, :])
            + third[here, :]
        )
        act, scaled, spread, slope = norm_gelu(pre, gain_one, bias_one)
        feats_ref[here, :] = act.astype(BF16)
        back, gain_term, bias_term = norm_back(
            cot_ref[here, :].astype(F32), gain_one, scaled, spread, slope
        )
        back = back.astype(BF16)
        back_one[here, :] = back
        back_f32[pl.ds(r + 8, chunk_rows), :] = back.astype(F32)
        return (sum_gain + fold_rows(gain_term), sum_bias + fold_rows(bias_term))

    zero_sum = jnp.zeros((8, width), F32)
    back_f32[0:8, :] = jnp.zeros((8, width), F32)
    back_f32[n_out + 8 :, :] = jnp.zeros((back_f32.shape[0] - n_out - 8, width), F32)
    sum_gain_one, sum_bias_one = lax.fori_loop(
        0, n_out // chunk_rows, layer_one, (zero_sum, zero_sum)
    )
    back_down[...] = back_f32[7 : 7 + n_even, :].astype(BF16)

    per_owner = 3 * width // 8 // n_dp

    def keep_pages(first_page, value):
        for i in range(width // 8):
            page = first_page + i
            d, j = page // per_owner, page % per_owner
            px, py, pc = d // (n_core * n_y), (d // n_core) % n_y, d % n_core
            at = ((pc * n_x + px) * n_y + py) * per_owner + j
            parts[at] = value[8 * i : 8 * i + 8, :].astype(BF16)

    keep_pages(0, dot(act_even[0:n_out, :], back_one[...], TN))
    keep_pages(width // 8, dot(act_odd[...], back_one[...], TN))
    keep_pages(2 * width // 8, dot(act_even[...], back_down[...], TN))

    half = n_x * n_y * per_owner
    x_part = n_y * per_owner
    core_copy = pltpu.make_async_remote_copy(
        src_ref=parts.at[pl.ds((1 - core) * half, half)],
        dst_ref=got_core,
        send_sem=core_sems.at[0],
        recv_sem=core_sems.at[1],
        device_id={"dp": dp_of(x, y, 1 - core)},
        device_id_type=MESH,
    )
    core_copy.start()

    def back_zero(r, n, upstream, scaled_ref, slope_ref, spread_ref, hi_ref, lo_ref):
        here = pl.ds(r, n)
        back, gain_term, bias_term = norm_back(
            upstream, gain_zero, scaled_ref[here, :], spread_ref[here, :], slope_ref[here, :]
        )
        hi = back.astype(BF16)
        hi_ref[here, :] = hi
        lo_ref[here, :] = (back - hi.astype(F32)).astype(BF16)
        return fold_rows(gain_term), fold_rows(bias_term)

    def back_even(i, carry):
        r = pl.multiple_of(i * chunk_rows, chunk_rows)
        here = pl.ds(r, chunk_rows)
        upstream = dot(back_one[here, :], w_ref[0:width, :], NT) + dot(
            back_down[here, :], w_ref[2 * width : 3 * width, :], NT
        )
        terms = back_zero(
            r, chunk_rows, upstream, scaled_even, slope_even, spread_even, hi_even, lo_even
        )
        return (carry[0] + terms[0], carry[1] + terms[1])

    def back_odd(i, carry):
        r = pl.multiple_of(i * chunk_rows, chunk_rows)
        here = pl.ds(r, chunk_rows)
        upstream = dot(back_one[here, :], w_ref[width : 2 * width, :], NT)
        terms = back_zero(
            r, chunk_rows, upstream, scaled_odd, slope_odd, spread_odd, hi_odd, lo_odd
        )
        return (carry[0] + terms[0], carry[1] + terms[1])

    sums = lax.fori_loop(0, n_out // chunk_rows, back_even, (zero_sum, zero_sum))
    upstream = (
        dot(back_down[n_out:n_even, :], w_ref[2 * width : 3 * width, :], NT) * keep
    )
    terms = back_zero(
        n_out, tail_rows, upstream, scaled_even, slope_even, spread_even, hi_even, lo_even
    )
    sums = (sums[0] + terms[0], sums[1] + terms[1])

    core_copy.wait_recv()
    mine = core * half

    def add_core(i, carry):
        at = pl.multiple_of(i * per_owner, per_owner)
        total = parts[pl.ds(mine + at, per_owner)].astype(F32) + got_core[
            pl.ds(at, per_owner)
        ].astype(F32)
        sum_core[pl.ds(at, per_owner)] = total.astype(BF16)
        return carry

    lax.fori_loop(0, half // per_owner, add_core, 0)

    def x_copy(k):
        peer = lax.rem(x + k, n_x)
        return pltpu.make_async_remote_copy(
            src_ref=sum_core.at[pl.ds(peer * x_part, x_part)],
            dst_ref=got_x.at[k],
            send_sem=x_send.at[k],
            recv_sem=x_recv.at[k],
            device_id={"dp": dp_of(peer, y, core)},
            device_id_type=MESH,
        )

    for k in range(1, n_x):
        x_copy(k).start()

    sums = lax.fori_loop(0, n_out // chunk_rows, back_odd, sums)

    grad_wz = (
        dot(patches[:, 0:128], hi_even[...], TN)
        + dot(patches[:, 0:128], lo_even[...], TN)
        + dot(patches[0:n_out, 128:256], hi_odd[...], TN)
        + dot(patches[0:n_out, 128:256], lo_odd[...], TN)
    )

    def row_sum(array):
        return jnp.sum(array, axis=0, keepdims=True)

    small[0, :, :] = grad_wz[0:8]
    small[1, 0:2, :] = grad_wz[8:10]
    small[1, 2:3, :] = row_sum(sums[0])
    small[1, 3:4, :] = row_sum(sums[1])
    small[1, 4:5, :] = row_sum(sum_gain_one)
    small[1, 5:6, :] = row_sum(sum_bias_one)
    small[1, 6:8, :] = jnp.zeros((2, width), F32)
    small_core_copy = pltpu.make_async_remote_copy(
        src_ref=small.at[1 - core],
        dst_ref=small_core,
        send_sem=sc_sems.at[0],
        recv_sem=sc_sems.at[1],
        device_id={"dp": dp_of(x, y, 1 - core)},
        device_id_type=MESH,
    )
    small_core_copy.start()
    small_core_copy.wait_recv()
    small_x[x] = small[core] + small_core[...]

    def sx_copy(k):
        return pltpu.make_async_remote_copy(
            src_ref=small_x.at[x],
            dst_ref=small_x.at[x],
            send_sem=sx_send.at[k],
            recv_sem=sx_recv.at[k],
            device_id={"dp": dp_of(lax.rem(x + k, n_x), y, core)},
            device_id_type=MESH,
        )

    for k in range(1, n_x):
        sx_copy(k).start()

    for k in range(1, n_x):
        x_copy(k).wait_recv()

    def add_x(i, carry):
        at = pl.multiple_of(i * per_owner, per_owner)
        here = pl.ds(at, per_owner)
        total = sum_core[pl.ds(x * x_part + at, per_owner)].astype(F32)
        for k in range(1, n_x):
            total = total + got_x[k, here].astype(F32)
        sum_x[here] = total.astype(BF16)
        return carry

    lax.fori_loop(0, n_y, add_x, 0)

    def y_copy(k):
        peer = lax.rem(y + k, n_y)
        return pltpu.make_async_remote_copy(
            src_ref=sum_x.at[pl.ds(peer * per_owner, per_owner)],
            dst_ref=got_y.at[k],
            send_sem=y_send.at[k],
            recv_sem=y_recv.at[k],
            device_id={"dp": dp_of(x, peer, core)},
            device_id_type=MESH,
        )

    for k in range(1, n_y):
        y_copy(k).start()

    for k in range(1, n_x):
        sx_copy(k).wait_recv()
    total = small_x[0]
    for k in range(1, n_x):
        total = total + small_x[k]
    small_y[y] = total

    def sy_copy(k):
        return pltpu.make_async_remote_copy(
            src_ref=small_y.at[y],
            dst_ref=small_y.at[y],
            send_sem=sy_send.at[k],
            recv_sem=sy_recv.at[k],
            device_id={"dp": dp_of(x, lax.rem(y + k, n_y), core)},
            device_id_type=MESH,
        )

    for k in range(1, n_y):
        sy_copy(k).start()

    for k in range(1, n_y):
        y_copy(k).wait_recv()
    total = sum_x[pl.ds(y * per_owner, per_owner)].astype(F32)
    for k in range(1, n_y):
        total = total + got_y[k].astype(F32)
    got_z[z] = total.astype(BF16)

    def z_copy(k):
        return pltpu.make_async_remote_copy(
            src_ref=got_z.at[z],
            dst_ref=got_z.at[z],
            send_sem=z_send.at[k],
            recv_sem=z_recv.at[k],
            device_id={"seq": lax.rem(z + k, n_z)},
            device_id_type=MESH,
        )

    order_z = sorted(range(1, n_z), key=lambda k: -min(k, n_z - k))
    for k in order_z:
        z_copy(k).start()

    for k in range(1, n_y):
        sy_copy(k).wait_recv()
    total = small_y[0]
    for k in range(1, n_y):
        total = total + small_y[k]
    small_z[z] = total.astype(BF16)

    def sz_copy(k):
        return pltpu.make_async_remote_copy(
            src_ref=small_z.at[z],
            dst_ref=small_z.at[z],
            send_sem=sz_send.at[k],
            recv_sem=sz_recv.at[k],
            device_id={"seq": lax.rem(z + k, n_z)},
            device_id_type=MESH,
        )

    for k in order_z:
        sz_copy(k).start()

    for k in range(1, n_z):
        z_copy(k).wait_recv()
    total = got_z[0].astype(F32)
    for k in range(1, n_z):
        total = total + got_z[k].astype(F32)
    for j in range(per_owner):
        grad_ref[8 * j : 8 * j + 8, :] = total[j]

    for k in range(1, n_z):
        sz_copy(k).wait_recv()
    total = small_z[0].astype(F32)
    for k in range(1, n_z):
        total = total + small_z[k].astype(F32)
    small_half[...] = total
    full_copy = pltpu.make_async_remote_copy(
        src_ref=small_half,
        dst_ref=small_full.at[core],
        send_sem=sf_sems.at[0],
        recv_sem=sf_sems.at[1],
        device_id={"dp": dp_of(x, y, 1 - core)},
        device_id_type=MESH,
    )
    full_copy.start()
    small_full[core] = total
    full_copy.wait_recv()
    gwz_ref[0:8, :] = small_full[0]
    rest = small_full[1]
    gwz_ref[8:10, :] = rest[0:2]
    ggz_ref[...] = rest[2:3]
    gbz_ref[...] = rest[3:4]
    gg1_ref[...] = rest[4:5]
    gb1_ref[...] = rest[5:6]

    def sent_msg(k, carry):
        msg_copy(k).wait_send()
        return carry

    lax.fori_loop(1, n_dp, sent_msg, 0)
    rim_copy.wait_send()
    core_copy.wait_send()
    small_core_copy.wait_send()
    full_copy.wait_send()
    for k in range(1, n_x):
        x_copy(k).wait_send()
        sx_copy(k).wait_send()
    for k in range(1, n_y):
        y_copy(k).wait_send()
        sy_copy(k).wait_send()
    for k in range(1, n_z):
        z_copy(k).wait_send()
        sz_copy(k).wait_send()


def on_device(n_dp, n_z, audio, send, place, cot, conv_zero, conv_one, gz, bz, g1, b1):
    n_x = n_dp // (n_core * n_y)
    n_rows, n_out, width = audio.shape[1], cot.shape[1], cot.shape[2]
    n_even = n_out + tail_rows
    per_owner = 3 * width // 8 // n_dp
    pages = 3 * width // 8
    vmem = lambda *shape, dtype=F32: pltpu.VMEM(shape, dtype)
    dma = lambda n: pltpu.SemaphoreType.DMA((n,))
    scratch = [
        vmem(n_dp, 1, lanes),
        vmem(n_dp, 1, lanes),
        vmem(8, lanes),
        vmem(8, lanes),
        vmem(n_rows + 16, lanes),
        vmem(n_even, lanes, dtype=BF16),
        vmem(128, width, dtype=BF16),
        vmem(n_even, width, dtype=BF16),
        vmem(n_out, width, dtype=BF16),
        vmem(n_even, width),
        vmem(n_out, width),
        vmem(n_even, width),
        vmem(n_out, width),
        vmem(n_even, 1),
        vmem(n_out, 1),
        vmem(n_even, width),
        vmem(n_out, width, dtype=BF16),
        vmem(n_out + 32, width),
        vmem(n_even, width, dtype=BF16),
        vmem(n_even, width, dtype=BF16),
        vmem(n_even, width, dtype=BF16),
        vmem(n_out, width, dtype=BF16),
        vmem(n_out, width, dtype=BF16),
        vmem(pages, 8, width, dtype=BF16),
        vmem(pages // 2, 8, width, dtype=BF16),
        vmem(pages // 2, 8, width, dtype=BF16),
        vmem(n_x, n_y * per_owner, 8, width, dtype=BF16),
        vmem(n_y * per_owner, 8, width, dtype=BF16),
        vmem(n_y, per_owner, 8, width, dtype=BF16),
        vmem(8, width),
        vmem(n_z, per_owner, 8, width, dtype=BF16),
        vmem(2, 8, width),
        vmem(8, width),
        vmem(n_x, 8, width),
        vmem(n_y, 8, width),
        vmem(n_z, 8, width, dtype=BF16),
        vmem(8, width),
        vmem(2, 8, width),
        dma(n_dp),
        dma(n_dp),
        dma(2),
        dma(2),
        dma(n_x),
        dma(n_x),
        dma(n_y),
        dma(n_y),
        dma(n_z),
        dma(n_z),
        dma(2),
        dma(n_x),
        dma(n_x),
        dma(n_y),
        dma(n_y),
        dma(n_z),
        dma(n_z),
        dma(2),
    ]
    row = jax.ShapeDtypeStruct((1, width), F32)
    outs = pl.pallas_call(
        functools.partial(kernel, (n_dp, n_x, n_z, n_rows, n_out, width)),
        out_shape=(
            jax.ShapeDtypeStruct((n_out, width), BF16),
            jax.ShapeDtypeStruct((3 * width // n_dp, width), F32),
            jax.ShapeDtypeStruct((10, width), F32),
            row,
            row,
            row,
            row,
        ),
        in_specs=[pl.BlockSpec(memory_space=pltpu.VMEM)] * 10,
        out_specs=(pl.BlockSpec(memory_space=pltpu.VMEM),) * 7,
        scratch_shapes=scratch,
        compiler_params=pltpu.CompilerParams(
            collective_id=0, has_side_effects=True, vmem_limit_bytes=56 * 2**20
        ),
    )(
        audio[0].T,
        send.reshape(1, -1),
        place.reshape(1, -1),
        cot[0],
        conv_zero,
        conv_one,
        gz[None],
        bz[None],
        g1[None],
        b1[None],
    )
    feats, grad, gwz, ggz, gbz, gg1, gb1 = outs
    return feats[None], grad, gwz, ggz[0], gbz[0], gg1[0], gb1[0]


def solution(mesh):
    placed = (
        P("dp", "seq", None),
        P("seq", "dp", None),
        P("seq", "dp", None),
        P("dp", "seq", None),
        P(),
        P(),
        P(),
        P(),
        P(),
        P(),
    )
    return jax.shard_map(
        functools.partial(on_device, mesh.shape["dp"], mesh.shape["seq"]),
        mesh=mesh,
        in_specs=placed,
        out_specs=(P("dp", "seq", None), P("dp", None), P(), P(), P(), P(), P()),
        check_vma=False,
    )
```

time: 261 us -> 94.5 us (0.36)
  blocking collectives: 124 us -> 0 us
  Pallas kernels: 0 us -> 83.1 us
  waiting for transfers between devices: 46.3 us -> 0 us
  starting transfers between devices: 28.9 us -> 0 us
  other arithmetic: 27 us -> 0 us
  local copies, waits for them, and re-layouts: 24.3 us -> 9.62 us
  matrix products: 8.34 us -> 0 us
    all_to_all x1 -> x0, blocking collectives: 124 us -> none  [sent_and_summed(): parts = lax.all_to_all(in_blocks(array, dim, count), axis, 0, 0, tiled=True)]
    pallas_call x0 -> x1, Pallas kernels: none -> 83.1 us  [on_device(): pl.pallas_call(functools.partial(kernel, (n_dp, n_x, n_z, n_rows, n_out,...]
    all_to_all x2 -> x0, waiting for transfers between devices: 43.3 us -> none  [the longest x1 36.8 us: from_everyone(): lax.all_to_all(jnp.broadcast_to(array[None], (count, *array.shape)), axis...]
    all_to_all x2 -> x0, starting transfers between devices: 27.6 us -> none  [the longest x1 14.6 us: on_device(): lax.all_to_all(outgoing, 'dp', split_axis=0, concat_axis=0, tiled=True)]
    reduce_sum x6 -> x0, other arithmetic: 11.6 us -> none  [the longest x2 8.02 us: norm_backward(): grad_gain = jnp.sum(inner_grad * scaled, axis=0)]
    dot_general x11 -> x0, matrix products: 8.34 us -> none  [the longest x1 1.5 us: layer_one(): jnp.dot(first_tap.T, back_one, preferred_element_type=jnp.float32)]
    slice x12 -> x0, local copies, waits for them, and re-layouts: 6.4 us -> none  [the longest x1 1.5 us: layer_one(): second_tap = frame_pairs[:, 1]]
    convert_element_type x2 -> x0, other arithmetic: 6.06 us -> none  [the longest x1 5.77 us: on_device(): frames_in = act_zero.astype(jnp.bfloat16)]
  transfers between devices with their start and end apart: 3 -> 0, of which waited for: 3 -> 0; matrix products, arithmetic and copies ran while one was open for 2% -> 0% of each run, Pallas kernels for 0% -> 0%
where the time goes in v1:
time: 94.5 us; the launch traced here: 93.4 us
  Pallas kernels  83.1 us (88%)
  local copies, waits for them, and re-layouts  9.62 us (10%)
    pallas_call x1, Pallas kernels, on_device(): pl.pallas_call(functools.partial(kernel, (n_dp, n_x, n_z, n_rows, n_out,...  83.1 us
    unnamed x7, local copies, waits for them, and re-layouts  9.62 us

profile of v1, /device:TPU:1, one launch (start us, length us, event | category | flops | bytes accessed | tf_op | source)
XLA Modules:
  0.0 93.4 jit_solution(16776937302290929255)
XLA Ops:
  0.6 83.1 %shard_map.153 = (bf16[512,512]{1,0:T(8,128)(2,1)}, f32[24,512]{1,0:T(8,128)}, f32[10,512]{1,0:T(8,128)}, f32[1,512]{1,0:T(1,128)}, f32[1,512]{1,0:T(1,128)}, /*index=5*/f32[1,512]{1,0:T(1,128)}, f32[1,512]{1,0:T(1,128)}) custom-call(bf16[40,128]{1,0:T(8,128)(2,1)} %bitcast.17, s32[1,256]{1,0:T(1,128)} %bitcast.26, s32[1,128]{1,0:T(1,128)} %bitcast.27, ...), custom_call_target="tpu_custom_call" | custom-call | tf_op jit(solution)/shard_map/pallas_call | solution.py:662
  83.8 1.9 %copy.24 = bf16[1,512,512]{2,1,0:T(8,128)(2,1)} copy(bf16[1,512,512]{2,1,0:T(8,128)(2,1)} %bitcast.16) | data formatting | bytes 1048576
  85.7 1.4 %copy.25 = f32[24,512]{1,0:T(8,128)} copy(f32[24,512]{1,0:T(8,128)} %get-tuple-element.29) | data formatting | bytes 98304
  87.1 1.4 %copy.26 = f32[10,512]{1,0:T(8,128)} copy(f32[10,512]{1,0:T(8,128)} %get-tuple-element.30) | data formatting | bytes 40960
  88.4 1.2 %copy.27 = f32[512]{0:T(512)} copy(f32[512]{0:T(512)} %bitcast.25) | data formatting | bytes 4096
  89.7 1.3 %copy.28 = f32[512]{0:T(512)} copy(f32[512]{0:T(512)} %bitcast.24) | data formatting | bytes 4096
  90.9 1.2 %copy.29 = f32[512]{0:T(512)} copy(f32[512]{0:T(512)} %bitcast.23) | data formatting | bytes 4096
  92.2 1.2 %copy.30 = f32[512]{0:T(512)} copy(f32[512]{0:T(512)} %bitcast.22) | data formatting | bytes 4096

commit v2 on v1

v2 whole, which is shorter than its diff:
```python
import functools

import jax
import jax.numpy as jnp
from jax import lax
from jax.experimental import pallas as pl
from jax.experimental.pallas import tpu as pltpu
from jax.sharding import PartitionSpec as P

MESH = pl.DeviceIdType.MESH
F32 = jnp.float32
BF16 = jnp.bfloat16
norm_eps = 1e-05
n_core = 2
n_y = 8
slots = 4
group = 64
lanes = slots * group
chunk_zero = 64
chunk_one = 128
chunk_back = 128
tail_rows = 16


def iota(shape, dim):
    return lax.broadcasted_iota(jnp.int32, shape, dim)


def one_hot(mask):
    return jnp.where(mask, 1.0, 0.0).astype(BF16)


def dot(a, b, dims=((1,), (0,))):
    return lax.dot_general(a, b, (dims, ((), ())), preferred_element_type=F32)


TN = ((0,), (0,))
NT = ((1,), (1,))


def norm_gelu(pre, gain, bias):
    center = pre - jnp.mean(pre, axis=-1, keepdims=True)
    spread = lax.rsqrt(jnp.mean(center * center, axis=-1, keepdims=True) + norm_eps)
    scaled = center * spread
    normed = scaled * gain + bias
    below = 0.5 + 0.5 * lax.erf(normed * 0.7071067811865476)
    act = normed * below
    slope = below + normed * (jnp.exp(-0.5 * normed * normed) * 0.3989422804014327)
    return act, scaled, spread, slope


def norm_back(upstream, gain, scaled, spread, slope):
    inner = upstream * slope
    pushed = inner * gain
    back = spread * (
        pushed
        - jnp.mean(pushed, axis=-1, keepdims=True)
        - scaled * jnp.mean(pushed * scaled, axis=-1, keepdims=True)
    )
    return back, inner * scaled, inner


def fold_rows(array):
    return jnp.sum(array.reshape(array.shape[0] // 8, 8, array.shape[1]), axis=0)


def kernel(
    sizes,
    audio_ref,
    send_ref,
    place_ref,
    cot_hbm,
    wz_ref,
    w_hbm,
    gz_ref,
    bz_ref,
    g1_ref,
    b1_ref,
    feats_hbm,
    grad_ref,
    small_full,
    cot_ref,
    w_ref,
    feats_ref,
    msg,
    got_msg,
    arr,
    own_row,
    rim,
    samples,
    patches,
    wz_pad,
    act_even,
    act_odd,
    scaled_even,
    scaled_odd,
    slope_even,
    slope_odd,
    spread_even,
    spread_odd,
    third,
    back_one,
    back_f32,
    back_down,
    hi_even,
    lo_even,
    hi_odd,
    lo_odd,
    parts,
    got_core,
    sum_core,
    got_x,
    sum_x,
    got_y,
    got_z,
    small,
    small_core,
    small_x,
    small_y,
    small_z,
    small_half,
    load_sems,
    near_send,
    near_recv,
    far_send,
    far_recv,
    rim_sems,
    core_send,
    core_recv,
    x_send,
    x_recv,
    y_send,
    y_recv,
    z_send,
    z_recv,
    sc_sems,
    sx_send,
    sx_recv,
    sy_send,
    sy_recv,
    sz_send,
    sz_recv,
    sf_sems,
):
    n_dp, n_x, n_z, n_rows, n_out, width = sizes
    n_even = n_out + tail_rows
    me = lax.axis_index("dp")
    z = lax.axis_index("seq")
    core = lax.rem(me, n_core)
    y = lax.rem(me // n_core, n_y)
    x = me // (n_core * n_y)

    def dp_of(px, py, pc):
        return (px * n_y + py) * n_core + pc

    n_near = n_x * n_core
    near = x * n_core + core

    def near_peer(k):
        at = lax.rem(near + k, n_near)
        return at, dp_of(at // n_core, y, lax.rem(at, n_core))

    def y_peer(k):
        at = lax.rem(y + k, n_y)
        return at, dp_of(x, at, core)

    barrier = pltpu.get_barrier_semaphore()

    def greet(axis, device):
        pl.semaphore_signal(barrier, inc=1, device_id={axis: device}, device_id_type=MESH)

    for k in range(1, n_near):
        greet("dp", near_peer(k)[1])
    for k in range(1, n_y):
        greet("dp", y_peer(k)[1])
    for k in range(1, n_z):
        greet("seq", lax.rem(z + k, n_z))

    load_w = pltpu.make_async_copy(w_hbm, w_ref, load_sems.at[0])
    load_cot = pltpu.make_async_copy(cot_hbm, cot_ref, load_sems.at[1])
    load_w.start()
    load_cot.start()

    spread_lanes = one_hot(
        jnp.bitwise_and(iota((40, lanes), 1), group - 1) == iota((40, lanes), 0)
    )
    blocks = dot(audio_ref[...], spread_lanes, TN).astype(BF16)
    chosen = one_hot(iota((n_rows, n_dp * slots), 0) == send_ref[...])
    picked = dot(chosen, blocks, TN)
    slot_of = jnp.bitwise_and(iota((n_dp * slots, lanes), 0), slots - 1)
    lane_group = lax.shift_right_logical(iota((n_dp * slots, lanes), 1), 6)
    in_group = slot_of == lane_group
    picked = jnp.where(in_group, picked, 0.0).astype(BF16)
    bit_y = n_y.bit_length() - 1

    def of_slot(shape, dim):
        device = lax.shift_right_logical(iota(shape, dim), 2)
        at_core = jnp.bitwise_and(device, n_core - 1)
        at_y = jnp.bitwise_and(lax.shift_right_logical(device, 1), n_y - 1)
        return lax.shift_right_logical(device, 1 + bit_y) * n_core + at_core, at_y

    slot_near, slot_y = of_slot((n_dp, n_dp * slots), 1)
    gather_dest = one_hot(slot_near * n_y + slot_y == iota((n_dp, n_dp * slots), 0))
    message = dot(gather_dest, picked)
    for d in range(n_dp):
        msg[d // n_y, d % n_y] = message[d : d + 1]

    pl.semaphore_wait(barrier, n_near - 1 + n_y - 1 + n_z - 1)

    def near_copy(k):
        at, device = near_peer(k)
        return pltpu.make_async_remote_copy(
            src_ref=msg.at[at],
            dst_ref=got_msg.at[near],
            send_sem=near_send.at[k],
            recv_sem=near_recv.at[k],
            device_id={"dp": device},
            device_id_type=MESH,
        )

    for k in range(1, n_near):
        near_copy(k).start()
    got_msg[near] = msg[near]

    wz_pad[...] = jnp.zeros_like(wz_pad)
    wz_pad[0:10, :] = wz_ref[...]
    gain_zero, bias_zero = gz_ref[...], bz_ref[...]
    gain_one, bias_one = g1_ref[...], b1_ref[...]
    keep = jnp.where(z < n_z - 1, 1.0, 0.0).astype(F32)
    placed = one_hot(iota((n_dp * slots, n_rows), 0) == place_ref[...])
    slot_near, slot_y = of_slot((n_dp * slots, n_dp), 0)
    spread_slots = one_hot(slot_y * n_near + slot_near == iota((n_dp * slots, n_dp), 1))
    lane_in, lane_out = iota((lanes, lanes), 0), iota((lanes, lanes), 1)
    sample_in = jnp.bitwise_and(lane_in, group - 1)
    sample_out = jnp.bitwise_and(lane_out, group - 1)
    fold_here = one_hot((sample_in == sample_out) & (sample_out < 40))
    fold_next = one_hot((sample_in + 40 == sample_out) & (sample_out < 45))
    row_id = iota((n_out, n_rows), 0)
    widen = one_hot(lax.shift_right_logical(row_id, 2) == iota((n_out, n_rows), 1))
    phase = jnp.bitwise_and(iota((n_out, lanes), 0), 3)
    own_phase = phase == lax.shift_right_logical(iota((n_out, lanes), 1), 6)
    tap = sample_in - 10 * lax.shift_right_logical(lane_in, 6)
    wanted = jnp.where(lane_out < 128, lane_out, lane_out - 128 + 5)
    limit = jnp.where(lane_out < 128, 10, 15)
    to_patch = one_hot((tap == wanted) & (wanted < limit))
    edge_from = jnp.where(lane_out < 128, lane_out, lane_out - 133)
    edge_limit = jnp.where(lane_out < 128, 10, 5)
    to_edge = one_hot((sample_in == edge_from) & (edge_from < edge_limit))

    for k in range(1, n_near):
        near_copy(k).wait_recv()

    def far_copy(k):
        at, device = y_peer(k)
        return pltpu.make_async_remote_copy(
            src_ref=got_msg.at[:, at],
            dst_ref=arr.at[y],
            send_sem=far_send.at[k],
            recv_sem=far_recv.at[k],
            device_id={"dp": device},
            device_id_type=MESH,
        )

    order_y = sorted(range(1, n_y), key=lambda k: -min(k, n_y - k))
    order_z = sorted(range(1, n_z), key=lambda k: -min(k, n_z - k))
    for k in order_y:
        far_copy(k).start()
    arr[y] = got_msg[:, y]
    for k in range(1, n_y):
        far_copy(k).wait_recv()

    received = jnp.concatenate(
        [arr[s // n_near, s % n_near] for s in range(n_dp)], axis=0
    ).astype(BF16)
    by_slot = dot(spread_slots, received)
    by_slot = jnp.where(in_group, by_slot, 0.0).astype(BF16)
    ordered = dot(placed, by_slot, TN)
    own_row[...] = dot(ordered[0:8].astype(BF16), to_edge)
    rim_copy = pltpu.make_async_remote_copy(
        src_ref=own_row,
        dst_ref=rim,
        send_sem=rim_sems.at[0],
        recv_sem=rim_sems.at[1],
        device_id={"seq": lax.rem(z + n_z - 1, n_z)},
        device_id_type=MESH,
    )
    rim_copy.start()
    samples[0:n_rows, :] = ordered
    samples[n_rows : n_rows + 8, :] = jnp.zeros((8, lanes), F32)
    wide = dot(samples[0:n_rows, :].astype(BF16), fold_here) + dot(
        samples[1 : n_rows + 1, :].astype(BF16), fold_next
    )
    rows = dot(widen, wide.astype(BF16))
    rows = jnp.where(own_phase, rows, 0.0).astype(BF16)
    patches[0:n_out, :] = dot(rows, to_patch).astype(BF16)

    def forward_even(r, n):
        pre = dot(patches[pl.ds(r, n), 0:128], wz_pad[...])
        act, scaled, spread, slope = norm_gelu(pre, gain_zero, bias_zero)
        scaled_even[pl.ds(r, n), :] = scaled
        slope_even[pl.ds(r, n), :] = slope
        spread_even[pl.ds(r, n), :] = spread
        return act

    def forward_odd(r, n):
        pre = dot(patches[pl.ds(r, n), 128:256], wz_pad[...])
        act, scaled, spread, slope = norm_gelu(pre, gain_zero, bias_zero)
        act_odd[pl.ds(r, n), :] = act.astype(BF16)
        scaled_odd[pl.ds(r, n), :] = scaled
        slope_odd[pl.ds(r, n), :] = slope
        spread_odd[pl.ds(r, n), :] = spread

    def forward_zero(i, carry):
        r = pl.multiple_of(i * chunk_zero, chunk_zero)
        act_even[pl.ds(r, chunk_zero), :] = forward_even(r, chunk_zero).astype(BF16)
        forward_odd(r, chunk_zero)
        return carry

    lax.fori_loop(0, n_out // chunk_zero, forward_zero, 0)

    rim_copy.wait_recv()
    edge = rim[0:1, :] * keep
    tail_id = iota((tail_rows, 128), 0)
    last = pl.ds(n_out - tail_rows, tail_rows)
    patches[last, 128:256] = (
        patches[last, 128:256].astype(F32)
        + jnp.where(tail_id == tail_rows - 1, edge[:, 128:256], 0.0)
    ).astype(BF16)
    patches[n_out:n_even, 0:128] = jnp.where(tail_id == 0, edge[:, 0:128], 0.0).astype(BF16)
    forward_odd(n_out - tail_rows, tail_rows)
    act_even[n_out:n_even, :] = (forward_even(n_out, tail_rows) * keep).astype(BF16)
    load_w.wait()

    third[...] = dot(act_even[...], w_ref[2 * width : 3 * width, :])
    for r in range(0, n_out, 64):
        third[r : r + 64, :] = third[r + 1 : r + 65, :]
    load_cot.wait()

    def layer_one(i, carry):
        sum_gain, sum_bias = carry
        r = pl.multiple_of(i * chunk_one, chunk_one)
        here = pl.ds(r, chunk_one)
        pre = (
            dot(act_even[here, :], w_ref[0:width, :])
            + dot(act_odd[here, :], w_ref[width : 2 * width, :])
            + third[here, :]
        )
        act, scaled, spread, slope = norm_gelu(pre, gain_one, bias_one)
        feats_ref[here, :] = act.astype(BF16)
        back, gain_term, bias_term = norm_back(
            cot_ref[here, :].astype(F32), gain_one, scaled, spread, slope
        )
        back = back.astype(BF16)
        back_one[here, :] = back
        back_f32[pl.ds(r + 8, chunk_one), :] = back.astype(F32)
        return (sum_gain + fold_rows(gain_term), sum_bias + fold_rows(bias_term))

    zero_sum = jnp.zeros((8, width), F32)
    back_f32[0:8, :] = jnp.zeros((8, width), F32)
    back_f32[n_out + 8 :, :] = jnp.zeros((back_f32.shape[0] - n_out - 8, width), F32)
    sum_gain_one, sum_bias_one = lax.fori_loop(
        0, n_out // chunk_one, layer_one, (zero_sum, zero_sum)
    )
    back_down[...] = back_f32[7 : 7 + n_even, :].astype(BF16)

    keep_feats = pltpu.make_async_copy(feats_ref, feats_hbm, load_sems.at[2])
    keep_feats.start()

    per_owner = 3 * width // 8 // n_dp

    def keep_pages(first_page, value):
        for i in range(width // 8):
            page = first_page + i
            d, j = page // per_owner, page % per_owner
            px, py, pc = d // (n_core * n_y), (d // n_core) % n_y, d % n_core
            parts[j, pc, px * n_y + py] = value[8 * i : 8 * i + 8, :].astype(BF16)

    keep_pages(0, dot(act_even[0:n_out, :], back_one[...], TN))
    keep_pages(width // 8, dot(act_odd[...], back_one[...], TN))
    keep_pages(2 * width // 8, dot(act_even[...], back_down[...], TN))

    partner = dp_of(x, y, 1 - core)

    def core_copy(j):
        return pltpu.make_async_remote_copy(
            src_ref=parts.at[j, 1 - core],
            dst_ref=got_core.at[j],
            send_sem=core_send.at[j],
            recv_sem=core_recv.at[j],
            device_id={"dp": partner},
            device_id_type=MESH,
        )

    for j in range(per_owner):
        core_copy(j).start()

    def back_zero(r, n, upstream, scaled_ref, slope_ref, spread_ref, hi_ref, lo_ref):
        here = pl.ds(r, n)
        back, gain_term, bias_term = norm_back(
            upstream, gain_zero, scaled_ref[here, :], spread_ref[here, :], slope_ref[here, :]
        )
        hi = back.astype(BF16)
        hi_ref[here, :] = hi
        lo_ref[here, :] = (back - hi.astype(F32)).astype(BF16)
        return fold_rows(gain_term), fold_rows(bias_term)

    def back_even(i, carry):
        r = pl.multiple_of(i * chunk_back, chunk_back)
        here = pl.ds(r, chunk_back)
        upstream = dot(back_one[here, :], w_ref[0:width, :], NT) + dot(
            back_down[here, :], w_ref[2 * width : 3 * width, :], NT
        )
        terms = back_zero(
            r, chunk_back, upstream, scaled_even, slope_even, spread_even, hi_even, lo_even
        )
        return (carry[0] + terms[0], carry[1] + terms[1])

    def back_odd(i, carry):
        r = pl.multiple_of(i * chunk_back, chunk_back)
        here = pl.ds(r, chunk_back)
        upstream = dot(back_one[here, :], w_ref[width : 2 * width, :], NT)
        terms = back_zero(
            r, chunk_back, upstream, scaled_odd, slope_odd, spread_odd, hi_odd, lo_odd
        )
        return (carry[0] + terms[0], carry[1] + terms[1])

    sums = lax.fori_loop(0, n_out // chunk_back, back_even, (zero_sum, zero_sum))
    upstream = (
        dot(back_down[n_out:n_even, :], w_ref[2 * width : 3 * width, :], NT) * keep
    )
    terms = back_zero(
        n_out, tail_rows, upstream, scaled_even, slope_even, spread_even, hi_even, lo_even
    )
    sums = (sums[0] + terms[0], sums[1] + terms[1])

    def x_copy(j, k):
        peer = lax.rem(x + k, n_x)
        return pltpu.make_async_remote_copy(
            src_ref=sum_core.at[j, pl.ds(peer * n_y, n_y)],
            dst_ref=got_x.at[j, k],
            send_sem=x_send.at[j, k],
            recv_sem=x_recv.at[j, k],
            device_id={"dp": dp_of(peer, y, core)},
            device_id_type=MESH,
        )

    order_x = sorted(range(1, n_x), key=lambda k: -min(k, n_x - k))
    for j in range(per_owner):
        core_copy(j).wait_recv()

        def add_core(i, carry):
            here = pl.ds(i * n_y, n_y)
            total = parts[j, core, here].astype(F32) + got_core[j, here].astype(F32)
            sum_core[j, here] = total.astype(BF16)
            return carry

        lax.fori_loop(0, n_x, add_core, 0)
        for k in order_x:
            x_copy(j, k).start()

    sums = lax.fori_loop(0, n_out // chunk_back, back_odd, sums)

    grad_wz = (
        dot(patches[:, 0:128], hi_even[...], TN)
        + dot(patches[:, 0:128], lo_even[...], TN)
        + dot(patches[0:n_out, 128:256], hi_odd[...], TN)
        + dot(patches[0:n_out, 128:256], lo_odd[...], TN)
    )

    def row_sum(array):
        return jnp.sum(array, axis=0, keepdims=True)

    small[0, :, :] = grad_wz[0:8]
    small[1, 0:2, :] = grad_wz[8:10]
    small[1, 2:3, :] = row_sum(sums[0])
    small[1, 3:4, :] = row_sum(sums[1])
    small[1, 4:5, :] = row_sum(sum_gain_one)
    small[1, 5:6, :] = row_sum(sum_bias_one)
    small[1, 6:8, :] = jnp.zeros((2, width), F32)
    small_core_copy = pltpu.make_async_remote_copy(
        src_ref=small.at[1 - core],
        dst_ref=small_core,
        send_sem=sc_sems.at[0],
        recv_sem=sc_sems.at[1],
        device_id={"dp": partner},
        device_id_type=MESH,
    )
    small_core_copy.start()

    def share(buffer, at, sends, recvs, axis, device):
        def copy(k):
            return pltpu.make_async_remote_copy(
                src_ref=buffer.at[at],
                dst_ref=buffer.at[at],
                send_sem=sends.at[k],
                recv_sem=recvs.at[k],
                device_id={axis: device(k)},
                device_id_type=MESH,
            )

        return copy

    sx_copy = share(
        small_x, x, sx_send, sx_recv, "dp", lambda k: dp_of(lax.rem(x + k, n_x), y, core)
    )
    sy_copy = share(small_y, y, sy_send, sy_recv, "dp", lambda k: y_peer(k)[1])
    sz_copy = share(small_z, z, sz_send, sz_recv, "seq", lambda k: lax.rem(z + k, n_z))
    z_copies = [
        share(
            got_z.at[j], z, z_send.at[j], z_recv.at[j], "seq", lambda k: lax.rem(z + k, n_z)
        )
        for j in range(per_owner)
    ]

    def total_of(buffer, count):
        total = buffer[0].astype(F32)
        for k in range(1, count):
            total = total + buffer[k].astype(F32)
        return total

    def y_copy(j, k):
        peer, device = y_peer(k)
        return pltpu.make_async_remote_copy(
            src_ref=sum_x.at[j, peer],
            dst_ref=got_y.at[j, k],
            send_sem=y_send.at[j, k],
            recv_sem=y_recv.at[j, k],
            device_id={"dp": device},
            device_id_type=MESH,
        )

    for j in range(per_owner):
        for k in range(1, n_x):
            x_copy(j, k).wait_recv()
        total = sum_core[j, pl.ds(x * n_y, n_y)].astype(F32)
        for k in range(1, n_x):
            total = total + got_x[j, k].astype(F32)
        sum_x[j] = total.astype(BF16)
        for k in order_y:
            y_copy(j, k).start()
        if j == 0:
            small_core_copy.wait_recv()
            small_x[x] = small[core] + small_core[...]
            for k in order_x:
                sx_copy(k).start()

    for k in range(1, n_x):
        sx_copy(k).wait_recv()
    small_y[y] = total_of(small_x, n_x)
    for k in order_y:
        sy_copy(k).start()

    for j in range(per_owner):
        if j == per_owner - 1:
            for k in range(1, n_y):
                sy_copy(k).wait_recv()
            small_z[z] = total_of(small_y, n_y).astype(BF16)
            for k in order_z:
                sz_copy(k).start()
        for k in range(1, n_y):
            y_copy(j, k).wait_recv()
        total = sum_x[j, y].astype(F32)
        for k in range(1, n_y):
            total = total + got_y[j, k].astype(F32)
        got_z[j, z] = total.astype(BF16)
        for k in order_z:
            z_copies[j](k).start()

    def finish(j):
        for k in range(1, n_z):
            z_copies[j](k).wait_recv()
        grad_ref[8 * j : 8 * j + 8, :] = total_of(got_z.at[j], n_z)

    for j in range(per_owner - 1):
        finish(j)
    for k in range(1, n_z):
        sz_copy(k).wait_recv()
    total = total_of(small_z, n_z)
    small_half[...] = total
    full_copy = pltpu.make_async_remote_copy(
        src_ref=small_half,
        dst_ref=small_full.at[core],
        send_sem=sf_sems.at[0],
        recv_sem=sf_sems.at[1],
        device_id={"dp": partner},
        device_id_type=MESH,
    )
    full_copy.start()
    small_full[core] = total
    finish(per_owner - 1)
    full_copy.wait_recv()

    keep_feats.wait()
    rim_copy.wait_send()
    small_core_copy.wait_send()
    full_copy.wait_send()
    for k in range(1, n_near):
        near_copy(k).wait_send()
    for k in range(1, n_x):
        sx_copy(k).wait_send()
    for k in range(1, n_y):
        far_copy(k).wait_send()
        sy_copy(k).wait_send()
    for k in range(1, n_z):
        sz_copy(k).wait_send()
    for j in range(per_owner):
        core_copy(j).wait_send()
        for k in range(1, n_x):
            x_copy(j, k).wait_send()
        for k in range(1, n_y):
            y_copy(j, k).wait_send()
        for k in range(1, n_z):
            z_copies[j](k).wait_send()


def hand_out(
    feats_in, grad_in, small_ref, feats_ref, grad_ref, gwz_ref, ggz_ref, gbz_ref, gg1_ref, gb1_ref
):
    feats_ref[...] = feats_in[...]
    grad_ref[...] = grad_in[...]
    gwz_ref[0:8, :] = small_ref[0]
    rest = small_ref[1]
    gwz_ref[8:10, :] = rest[0:2]
    ggz_ref[...] = rest[2:3]
    gbz_ref[...] = rest[3:4]
    gg1_ref[...] = rest[4:5]
    gb1_ref[...] = rest[5:6]


def on_device(n_dp, n_z, audio, send, place, cot, conv_zero, conv_one, gz, bz, g1, b1):
    n_x = n_dp // (n_core * n_y)
    n_rows, n_out, width = audio.shape[1], cot.shape[1], cot.shape[2]
    n_even = n_out + tail_rows
    per_owner = 3 * width // 8 // n_dp
    n_near = n_x * n_core
    vmem = lambda *shape, dtype=F32: pltpu.VMEM(shape, dtype)
    page = lambda *shape: pltpu.VMEM((*shape, 8, width), BF16)
    dma = lambda *shape: pltpu.SemaphoreType.DMA(shape)
    scratch = [
        vmem(n_out, width, dtype=BF16),
        vmem(3 * width, width, dtype=BF16),
        vmem(n_out, width, dtype=BF16),
        vmem(n_near, n_y, 1, lanes),
        vmem(n_near, n_y, 1, lanes),
        vmem(n_y, n_near, 1, lanes),
        vmem(8, lanes),
        vmem(8, lanes),
        vmem(n_rows + 8, lanes),
        vmem(n_even, lanes, dtype=BF16),
        vmem(128, width, dtype=BF16),
        vmem(n_even, width, dtype=BF16),
        vmem(n_out, width, dtype=BF16),
        vmem(n_even, width),
        vmem(n_out, width),
        vmem(n_even, width),
        vmem(n_out, width),
        vmem(n_even, 1),
        vmem(n_out, 1),
        vmem(n_even, width),
        vmem(n_out, width, dtype=BF16),
        vmem(n_out + 32, width),
        vmem(n_even, width, dtype=BF16),
        vmem(n_even, width, dtype=BF16),
        vmem(n_even, width, dtype=BF16),
        vmem(n_out, width, dtype=BF16),
        vmem(n_out, width, dtype=BF16),
        page(per_owner, n_core, n_x * n_y),
        page(per_owner, n_x * n_y),
        page(per_owner, n_x * n_y),
        page(per_owner, n_x, n_y),
        page(per_owner, n_y),
        page(per_owner, n_y),
        page(per_owner, n_z),
        vmem(2, 8, width),
        vmem(8, width),
        vmem(n_x, 8, width),
        vmem(n_y, 8, width),
        page(n_z),
        vmem(8, width),
        dma(3),
        dma(n_near),
        dma(n_near),
        dma(n_y),
        dma(n_y),
        dma(2),
        dma(per_owner),
        dma(per_owner),
        dma(per_owner, n_x),
        dma(per_owner, n_x),
        dma(per_owner, n_y),
        dma(per_owner, n_y),
        dma(per_owner, n_z),
        dma(per_owner, n_z),
        dma(2),
        dma(n_x),
        dma(n_x),
        dma(n_y),
        dma(n_y),
        dma(n_z),
        dma(n_z),
        dma(2),
    ]
    row = jax.ShapeDtypeStruct((1, width), F32)
    in_vmem = pl.BlockSpec(memory_space=pltpu.VMEM)
    anywhere = pl.BlockSpec(memory_space=pl.ANY)
    feats, grad, small = pl.pallas_call(
        functools.partial(kernel, (n_dp, n_x, n_z, n_rows, n_out, width)),
        out_shape=(
            jax.ShapeDtypeStruct((n_out, width), BF16),
            jax.ShapeDtypeStruct((3 * width // n_dp, width), F32),
            jax.ShapeDtypeStruct((2, 8, width), F32),
        ),
        in_specs=[in_vmem, in_vmem, in_vmem, anywhere, in_vmem, anywhere, *[in_vmem] * 4],
        out_specs=(anywhere, in_vmem, in_vmem),
        scratch_shapes=scratch,
        compiler_params=pltpu.CompilerParams(
            collective_id=0, has_side_effects=True, vmem_limit_bytes=60 * 2**20
        ),
    )(
        audio[0].T,
        send.reshape(1, -1),
        place.reshape(1, -1),
        cot[0],
        conv_zero,
        conv_one,
        gz[None],
        bz[None],
        g1[None],
        b1[None],
    )
    feats, grad, gwz, ggz, gbz, gg1, gb1 = pl.pallas_call(
        hand_out,
        out_shape=(
            jax.ShapeDtypeStruct(feats.shape, feats.dtype),
            jax.ShapeDtypeStruct(grad.shape, grad.dtype),
            jax.ShapeDtypeStruct((10, width), F32),
            row,
            row,
            row,
            row,
        ),
        in_specs=[in_vmem] * 3,
        out_specs=(in_vmem,) * 7,
        compiler_params=pltpu.CompilerParams(vmem_limit_bytes=60 * 2**20),
    )(feats, grad, small)
    return feats[None], grad, gwz, ggz[0], gbz[0], gg1[0], gb1[0]


def solution(mesh):
    placed = (
        P("dp", "seq", None),
        P("seq", "dp", None),
        P("seq", "dp", None),
        P("dp", "seq", None),
        P(),
        P(),
        P(),
        P(),
        P(),
        P(),
    )
    return jax.shard_map(
        functools.partial(on_device, mesh.shape["dp"], mesh.shape["seq"]),
        mesh=mesh,
        in_specs=placed,
        out_specs=(P("dp", "seq", None), P("dp", None), P(), P(), P(), P(), P()),
        check_vma=False,
    )
```

time: 94.5 us -> 72 us (0.76)
  Pallas kernels: 83.1 us -> 71 us
  local copies, waits for them, and re-layouts: 9.62 us -> 0 us
    pallas_call x1, Pallas kernels: 83.1 us -> 69.1 us  [on_device(): pl.pallas_call(functools.partial(kernel, (n_dp, n_x, n_z, n_rows, n_out,...]
    unnamed x7 -> x0, local copies, waits for them, and re-layouts: 9.62 us -> none
    pallas_call x0 -> x1, Pallas kernels: none -> 1.91 us  [on_device(): pl.pallas_call(hand_out, out_shape=(jax.ShapeDtypeStruct(feats.shape, fea...]
where the time goes in v2:
time: 72 us; the launch traced here: 71.6 us
  Pallas kernels  71 us (99%)
    pallas_call x1, Pallas kernels, on_device(): pl.pallas_call(functools.partial(kernel, (n_dp, n_x, n_z, n_rows, n_out,...  69.1 us
    pallas_call x1, Pallas kernels, on_device(): pl.pallas_call(hand_out, out_shape=(jax.ShapeDtypeStruct(feats.shape, fea...  1.91 us

profile of v2, /device:TPU:1, one launch (start us, length us, event | category | flops | bytes accessed | tf_op | source)
XLA Modules:
  0.0 71.6 jit_solution(14429748675154466083)
XLA Ops:
  0.6 69.1 %shard_map.153 = (bf16[512,512]{1,0:T(8,128)(2,1)}, f32[24,512]{1,0:T(8,128)}, f32[2,8,512]{2,1,0:T(8,128)}) custom-call(bf16[40,128]{1,0:T(8,128)(2,1)} %bitcast.16, s32[1,256]{1,0:T(1,128)} %bitcast.21, s32[1,128]{1,0:T(1,128)} %bitcast.22, bf16[512,512]{1,0:T(8,128)(2,1)} %bitcast.15, bf16[10,512]{1,0:T(8,128)(2,1)} %wz_ref.1, bf16[1536,512]{1,0:T(8,128)(2,1)} %w_hbm.1, ...), custom_call_target="tpu_custom_call" | custom-call | tf_op jit(solution)/shard_map/pallas_call | solution.py:706
  69.7 1.9 %shard_map.154 = (bf16[512,512]{1,0:T(8,128)(2,1)}, f32[24,512]{1,0:T(8,128)}, f32[10,512]{1,0:T(8,128)}, f32[1,512]{1,0:T(1,128)}, f32[1,512]{1,0:T(1,128)}, /*index=5*/f32[1,512]{1,0:T(1,128)}, f32[1,512]{1,0:T(1,128)}) custom-call(bf16[512,512]{1,0:T(8,128)(2,1)} %get-tuple-element.17.feats_in, f32[24,512]{1,0:T(8,128)} %get-tuple-element.18.grad_in, ...), custom_call_target="tpu_custom_call" | custom-call | tf_op jit(solution)/shard_map/pallas_call | solution.py:731

commit v3 on v2

--- a/solution.py
+++ b/solution.py
@@ -16,10 +16,11 @@
 slots = 4
 group = 64
 lanes = slots * group
-chunk_zero = 64
+chunk_zero = 128
 chunk_one = 128
 chunk_back = 128
 tail_rows = 16
+quarters = 4
 
 
 def iota(shape, dim):
@@ -112,6 +113,9 @@
     got_x,
     sum_x,
     got_y,
+    got_y_first,
+    sum_y_first,
+    got_x_second,
     got_z,
     small,
     small_core,
@@ -367,32 +371,36 @@
     keep_feats.start()
 
     per_owner = 3 * width // 8 // n_dp
-
-    def keep_pages(first_page, value):
+    cols = width // quarters
+    partner = dp_of(x, y, 1 - core)
+
+    def keep_pages(first_page, quarter, value):
         for i in range(width // 8):
             page = first_page + i
             d, j = page // per_owner, page % per_owner
             px, py, pc = d // (n_core * n_y), (d // n_core) % n_y, d % n_core
-            parts[j, pc, px * n_y + py] = value[8 * i : 8 * i + 8, :].astype(BF16)
-
-    keep_pages(0, dot(act_even[0:n_out, :], back_one[...], TN))
-    keep_pages(width // 8, dot(act_odd[...], back_one[...], TN))
-    keep_pages(2 * width // 8, dot(act_even[...], back_down[...], TN))
-
-    partner = dp_of(x, y, 1 - core)
-
-    def core_copy(j):
+            for q in range(2):
+                parts[quarter + q, pc, px, py, j] = value[
+                    8 * i : 8 * i + 8, q * cols : (q + 1) * cols
+                ].astype(BF16)
+
+    def core_copy(q):
         return pltpu.make_async_remote_copy(
-            src_ref=parts.at[j, 1 - core],
-            dst_ref=got_core.at[j],
-            send_sem=core_send.at[j],
-            recv_sem=core_recv.at[j],
+            src_ref=parts.at[q, 1 - core],
+            dst_ref=got_core.at[q],
+            send_sem=core_send.at[q],
+            recv_sem=core_recv.at[q],
             device_id={"dp": partner},
             device_id_type=MESH,
         )
 
-    for j in range(per_owner):
-        core_copy(j).start()
+    for q in range(0, quarters, 2):
+        here = slice(q * cols, (q + 2) * cols)
+        keep_pages(0, q, dot(act_even[0:n_out, :], back_one[:, here], TN))
+        keep_pages(width // 8, q, dot(act_odd[...], back_one[:, here], TN))
+        keep_pages(2 * width // 8, q, dot(act_even[...], back_down[:, here], TN))
+        core_copy(q).start()
+        core_copy(q + 1).start()
 
     def back_zero(r, n, upstream, scaled_ref, slope_ref, spread_ref, hi_ref, lo_ref):
         here = pl.ds(r, n)
@@ -424,7 +432,66 @@
         )
         return (carry[0] + terms[0], carry[1] + terms[1])
 
-    sums = lax.fori_loop(0, n_out // chunk_back, back_even, (zero_sum, zero_sum))
+    order_x = sorted(range(1, n_x), key=lambda k: -min(k, n_x - k))
+
+    def x_peer(k):
+        at = lax.rem(x + k, n_x)
+        return at, dp_of(at, y, core)
+
+    def send(src, dst, send_sem, recv_sem, axis, device):
+        return pltpu.make_async_remote_copy(
+            src_ref=src,
+            dst_ref=dst,
+            send_sem=send_sem,
+            recv_sem=recv_sem,
+            device_id={axis: device},
+            device_id_type=MESH,
+        )
+
+    def x_copy(q, k):
+        at, device = x_peer(k)
+        src, dst = (
+            (sum_y_first.at[at], got_x_second.at[k])
+            if q == 0
+            else (sum_core.at[q, at], got_x.at[q, k])
+        )
+        return send(src, dst, x_send.at[q, k], x_recv.at[q, k], "dp", device)
+
+    def y_copy(q, k):
+        at, device = y_peer(k)
+        src, dst = (
+            (sum_core.at[0, :, at], got_y_first.at[k])
+            if q == 0
+            else (sum_x.at[q, at], got_y.at[q, k])
+        )
+        return send(src, dst, y_send.at[q, k], y_recv.at[q, k], "dp", device)
+
+    def pair_sum(q):
+        core_copy(q).wait_recv()
+
+        def add_core(i, carry):
+            total = parts[q, core, i].astype(F32) + got_core[q, i].astype(F32)
+            sum_core[q, i] = total.astype(BF16)
+            return carry
+
+        lax.fori_loop(0, n_x, add_core, 0)
+        if q == 0:
+            for k in order_y:
+                y_copy(0, k).start()
+        else:
+            for k in order_x:
+                x_copy(q, k).start()
+
+    sums = back_even(0, (zero_sum, zero_sum))
+    pair_sum(0)
+    pair_sum(1)
+    n_chunks = n_out // chunk_back
+    if n_chunks > 1:
+        sums = back_even(1, sums)
+    pair_sum(2)
+    pair_sum(3)
+    for i in range(2, n_chunks):
+        sums = back_even(i, sums)
     upstream = (
         dot(back_down[n_out:n_even, :], w_ref[2 * width : 3 * width, :], NT) * keep
     )
@@ -432,33 +499,7 @@
         n_out, tail_rows, upstream, scaled_even, slope_even, spread_even, hi_even, lo_even
     )
     sums = (sums[0] + terms[0], sums[1] + terms[1])
-
-    def x_copy(j, k):
-        peer = lax.rem(x + k, n_x)
-        return pltpu.make_async_remote_copy(
-            src_ref=sum_core.at[j, pl.ds(peer * n_y, n_y)],
-            dst_ref=got_x.at[j, k],
-            send_sem=x_send.at[j, k],
-            recv_sem=x_recv.at[j, k],
-            device_id={"dp": dp_of(peer, y, core)},
-            device_id_type=MESH,
-        )
-
-    order_x = sorted(range(1, n_x), key=lambda k: -min(k, n_x - k))
-    for j in range(per_owner):
-        core_copy(j).wait_recv()
-
-        def add_core(i, carry):
-            here = pl.ds(i * n_y, n_y)
-            total = parts[j, core, here].astype(F32) + got_core[j, here].astype(F32)
-            sum_core[j, here] = total.astype(BF16)
-            return carry
-
-        lax.fori_loop(0, n_x, add_core, 0)
-        for k in order_x:
-            x_copy(j, k).start()
-
-    sums = lax.fori_loop(0, n_out // chunk_back, back_odd, sums)
+    sums = lax.fori_loop(0, n_chunks, back_odd, sums)
 
     grad_wz = (
         dot(patches[:, 0:128], hi_even[...], TN)
@@ -500,16 +541,14 @@
 
         return copy
 
-    sx_copy = share(
-        small_x, x, sx_send, sx_recv, "dp", lambda k: dp_of(lax.rem(x + k, n_x), y, core)
-    )
+    sx_copy = share(small_x, x, sx_send, sx_recv, "dp", lambda k: x_peer(k)[1])
     sy_copy = share(small_y, y, sy_send, sy_recv, "dp", lambda k: y_peer(k)[1])
     sz_copy = share(small_z, z, sz_send, sz_recv, "seq", lambda k: lax.rem(z + k, n_z))
     z_copies = [
         share(
-            got_z.at[j], z, z_send.at[j], z_recv.at[j], "seq", lambda k: lax.rem(z + k, n_z)
-        )
-        for j in range(per_owner)
+            got_z.at[q], z, z_send.at[q], z_recv.at[q], "seq", lambda k: lax.rem(z + k, n_z)
+        )
+        for q in range(quarters)
     ]
 
     def total_of(buffer, count):
@@ -518,76 +557,73 @@
             total = total + buffer[k].astype(F32)
         return total
 
-    def y_copy(j, k):
-        peer, device = y_peer(k)
-        return pltpu.make_async_remote_copy(
-            src_ref=sum_x.at[j, peer],
-            dst_ref=got_y.at[j, k],
-            send_sem=y_send.at[j, k],
-            recv_sem=y_recv.at[j, k],
-            device_id={"dp": device},
-            device_id_type=MESH,
-        )
-
-    for j in range(per_owner):
-        for k in range(1, n_x):
-            x_copy(j, k).wait_recv()
-        total = sum_core[j, pl.ds(x * n_y, n_y)].astype(F32)
-        for k in range(1, n_x):
-            total = total + got_x[j, k].astype(F32)
-        sum_x[j] = total.astype(BF16)
+    def plus_got(total, buffer, count):
+        total = total.astype(F32)
+        for k in range(1, count):
+            total = total + buffer[k].astype(F32)
+        return total.astype(BF16)
+
+    def got_all(copy, count):
+        for k in range(1, count):
+            copy(k).wait_recv()
+
+    def along_y(q):
+        got_all(functools.partial(x_copy, q), n_x)
+        sum_x[q] = plus_got(sum_core[q, x], got_x.at[q], n_x)
         for k in order_y:
-            y_copy(j, k).start()
-        if j == 0:
-            small_core_copy.wait_recv()
-            small_x[x] = small[core] + small_core[...]
-            for k in order_x:
-                sx_copy(k).start()
-
-    for k in range(1, n_x):
-        sx_copy(k).wait_recv()
+            y_copy(q, k).start()
+
+    def along_z(q):
+        if q == 0:
+            got_all(functools.partial(x_copy, 0), n_x)
+            got_z[0, z] = plus_got(sum_y_first[x], got_x_second, n_x)
+        else:
+            got_all(functools.partial(y_copy, q), n_y)
+            got_z[q, z] = plus_got(sum_x[q, y], got_y.at[q], n_y)
+        for k in order_z:
+            z_copies[q](k).start()
+
+    def finish(q):
+        got_all(z_copies[q], n_z)
+        total = total_of(got_z.at[q], n_z)
+        for j in range(per_owner):
+            grad_ref[8 * j : 8 * j + 8, q * cols : (q + 1) * cols] = total[j]
+
+    along_y(1)
+    small_core_copy.wait_recv()
+    small_z[z] = (small[core] + small_core[...]).astype(BF16)
+    for k in order_z:
+        sz_copy(k).start()
+    along_y(2)
+    got_all(functools.partial(y_copy, 0), n_y)
+    sum_y_first[...] = plus_got(sum_core[0, :, y], got_y_first, n_y)
+    for k in order_x:
+        x_copy(0, k).start()
+    along_y(3)
+    along_z(1)
+    along_z(0)
+    got_all(sz_copy, n_z)
+    small_x[x] = total_of(small_z, n_z)
+    for k in order_x:
+        sx_copy(k).start()
+    along_z(2)
+    got_all(sx_copy, n_x)
     small_y[y] = total_of(small_x, n_x)
     for k in order_y:
         sy_copy(k).start()
-
-    for j in range(per_owner):
-        if j == per_owner - 1:
-            for k in range(1, n_y):
-                sy_copy(k).wait_recv()
-            small_z[z] = total_of(small_y, n_y).astype(BF16)
-            for k in order_z:
-                sz_copy(k).start()
-        for k in range(1, n_y):
-            y_copy(j, k).wait_recv()
-        total = sum_x[j, y].astype(F32)
-        for k in range(1, n_y):
-            total = total + got_y[j, k].astype(F32)
-        got_z[j, z] = total.astype(BF16)
-        for k in order_z:
-            z_copies[j](k).start()
-
-    def finish(j):
-        for k in range(1, n_z):
-            z_copies[j](k).wait_recv()
-        grad_ref[8 * j : 8 * j + 8, :] = total_of(got_z.at[j], n_z)
-
-    for j in range(per_owner - 1):
-        finish(j)
-    for k in range(1, n_z):
-        sz_copy(k).wait_recv()
-    total = total_of(small_z, n_z)
+    along_z(3)
+    finish(1)
+    finish(0)
+    got_all(sy_copy, n_y)
+    total = total_of(small_y, n_y)
     small_half[...] = total
-    full_copy = pltpu.make_async_remote_copy(
-        src_ref=small_half,
-        dst_ref=small_full.at[core],
-        send_sem=sf_sems.at[0],
-        recv_sem=sf_sems.at[1],
-        device_id={"dp": partner},
-        device_id_type=MESH,
+    full_copy = send(
+        small_half, small_full.at[core], sf_sems.at[0], sf_sems.at[1], "dp", partner
     )
     full_copy.start()
     small_full[core] = total
-    finish(per_owner - 1)
+    finish(2)
+    finish(3)
     full_copy.wait_recv()
 
     keep_feats.wait()
@@ -603,14 +639,14 @@
         sy_copy(k).wait_send()
     for k in range(1, n_z):
         sz_copy(k).wait_send()
-    for j in range(per_owner):
-        core_copy(j).wait_send()
+    for q in range(quarters):
+        core_copy(q).wait_send()
         for k in range(1, n_x):
-            x_copy(j, k).wait_send()
+            x_copy(q, k).wait_send()
         for k in range(1, n_y):
-            y_copy(j, k).wait_send()
+            y_copy(q, k).wait_send()
         for k in range(1, n_z):
-            z_copies[j](k).wait_send()
+            z_copies[q](k).wait_send()
 
 
 def hand_out(
@@ -634,7 +670,7 @@
     per_owner = 3 * width // 8 // n_dp
     n_near = n_x * n_core
     vmem = lambda *shape, dtype=F32: pltpu.VMEM(shape, dtype)
-    page = lambda *shape: pltpu.VMEM((*shape, 8, width), BF16)
+    page = lambda *shape: pltpu.VMEM((*shape, per_owner, 8, width // quarters), BF16)
     dma = lambda *shape: pltpu.SemaphoreType.DMA(shape)
     scratch = [
         vmem(n_out, width, dtype=BF16),
@@ -664,18 +700,21 @@
         vmem(n_even, width, dtype=BF16),
         vmem(n_out, width, dtype=BF16),
         vmem(n_out, width, dtype=BF16),
-        page(per_owner, n_core, n_x * n_y),
-        page(per_owner, n_x * n_y),
-        page(per_owner, n_x * n_y),
-        page(per_owner, n_x, n_y),
-        page(per_owner, n_y),
-        page(per_owner, n_y),
-        page(per_owner, n_z),
+        page(quarters, n_core, n_x, n_y),
+        page(quarters, n_x, n_y),
+        page(quarters, n_x, n_y),
+        page(quarters, n_x, n_y),
+        page(quarters, n_y),
+        page(quarters, n_y),
+        page(n_y, n_x),
+        page(n_x),
+        page(n_x),
+        page(quarters, n_z),
         vmem(2, 8, width),
         vmem(8, width),
         vmem(n_x, 8, width),
         vmem(n_y, 8, width),
-        page(n_z),
+        vmem(n_z, 8, width, dtype=BF16),
         vmem(8, width),
         dma(3),
         dma(n_near),
@@ -683,14 +722,14 @@
         dma(n_y),
         dma(n_y),
         dma(2),
-        dma(per_owner),
-        dma(per_owner),
-        dma(per_owner, n_x),
-        dma(per_owner, n_x),
-        dma(per_owner, n_y),
-        dma(per_owner, n_y),
-        dma(per_owner, n_z),
-        dma(per_owner, n_z),
+        dma(quarters),
+        dma(quarters),
+        dma(quarters, n_x),
+        dma(quarters, n_x),
+        dma(quarters, n_y),
+        dma(quarters, n_y),
+        dma(quarters, n_z),
+        dma(quarters, n_z),
         dma(2),
         dma(n_x),
         dma(n_x),

time: 72 us -> 66.9 us (0.929)
  Pallas kernels: 71 us -> 66 us
    pallas_call x1, Pallas kernels: 69.1 us -> 64.1 us  [on_device(): pl.pallas_call(functools.partial(kernel, (n_dp, n_x, n_z, n_rows, n_out,...]
where the time goes in v3:
time: 66.9 us; the launch traced here: 66.7 us
  Pallas kernels  66 us (99%)
    pallas_call x1, Pallas kernels, on_device(): pl.pallas_call(functools.partial(kernel, (n_dp, n_x, n_z, n_rows, n_out,...  64.1 us
    pallas_call x1, Pallas kernels, on_device(): pl.pallas_call(hand_out, out_shape=(jax.ShapeDtypeStruct(feats.shape, fea...  1.91 us

profile of v3, /device:TPU:1, one launch (start us, length us, event | category | flops | bytes accessed | tf_op | source)
XLA Modules:
  0.0 66.7 jit_solution(5925726204164290429)
XLA Ops:
  0.6 64.1 %shard_map.153 = (bf16[512,512]{1,0:T(8,128)(2,1)}, f32[24,512]{1,0:T(8,128)}, f32[2,8,512]{2,1,0:T(8,128)}) custom-call(bf16[40,128]{1,0:T(8,128)(2,1)} %bitcast.16, s32[1,256]{1,0:T(1,128)} %bitcast.21, s32[1,128]{1,0:T(1,128)} %bitcast.22, bf16[512,512]{1,0:T(8,128)(2,1)} %bitcast.15, bf16[10,512]{1,0:T(8,128)(2,1)} %wz_ref.1, bf16[1536,512]{1,0:T(8,128)(2,1)} %w_hbm.1, ...), custom_call_target="tpu_custom_call" | custom-call | tf_op jit(solution)/shard_map/pallas_call | solution.py:745
  64.8 1.9 %shard_map.154 = (bf16[512,512]{1,0:T(8,128)(2,1)}, f32[24,512]{1,0:T(8,128)}, f32[10,512]{1,0:T(8,128)}, f32[1,512]{1,0:T(1,128)}, f32[1,512]{1,0:T(1,128)}, /*index=5*/f32[1,512]{1,0:T(1,128)}, f32[1,512]{1,0:T(1,128)}) custom-call(bf16[512,512]{1,0:T(8,128)(2,1)} %get-tuple-element.17.feats_in, f32[24,512]{1,0:T(8,128)} %get-tuple-element.18.grad_in, ...), custom_call_target="tpu_custom_call" | custom-call | tf_op jit(solution)/shard_map/pallas_call | solution.py:770

commit v4 on v3

--- a/solution.py
+++ b/solution.py
@@ -67,19 +67,27 @@
 
 def kernel(
     sizes,
+    audio_hbm,
+    send_hbm,
+    place_hbm,
+    cot_hbm,
+    wz_hbm,
+    w_hbm,
+    gz_hbm,
+    bz_hbm,
+    g1_hbm,
+    b1_hbm,
+    feats_hbm,
+    grad_ref,
+    small_full,
     audio_ref,
     send_ref,
     place_ref,
-    cot_hbm,
     wz_ref,
-    w_hbm,
     gz_ref,
     bz_ref,
     g1_ref,
     b1_ref,
-    feats_hbm,
-    grad_ref,
-    small_full,
     cot_ref,
     w_ref,
     feats_ref,
@@ -145,6 +153,8 @@
     sz_send,
     sz_recv,
     sf_sems,
+    y_ready,
+    z_ready,
 ):
     n_dp, n_x, n_z, n_rows, n_out, width = sizes
     n_even = n_out + tail_rows
@@ -173,21 +183,58 @@
     def greet(axis, device):
         pl.semaphore_signal(barrier, inc=1, device_id={axis: device}, device_id_type=MESH)
 
+    y_next = sorted({1, n_y - 1})
+    z_next = sorted({1, n_z - 1})
+    for k in z_next:
+        greet("seq", lax.rem(z + k, n_z))
+    for k in y_next:
+        greet("dp", y_peer(k)[1])
     for k in range(1, n_near):
         greet("dp", near_peer(k)[1])
-    for k in range(1, n_y):
-        greet("dp", y_peer(k)[1])
-    for k in range(1, n_z):
-        greet("seq", lax.rem(z + k, n_z))
-
-    load_w = pltpu.make_async_copy(w_hbm, w_ref, load_sems.at[0])
-    load_cot = pltpu.make_async_copy(cot_hbm, cot_ref, load_sems.at[1])
-    load_w.start()
-    load_cot.start()
+
+    def rounds(count, ready, axis, device):
+        for _ in range(2, count // 2 + 1):
+            for side, k in enumerate((1, count - 1)):
+                pl.semaphore_signal(
+                    ready.at[side], inc=1, device_id={axis: device(k)}, device_id_type=MESH
+                )
+            yield
+            for side in range(2):
+                pl.semaphore_wait(ready.at[side], 1)
+
+    y_rounds = rounds(n_y, y_ready, "dp", lambda k: y_peer(k)[1])
+    z_rounds = rounds(n_z, z_ready, "seq", lambda k: lax.rem(z + k, n_z))
+
+    def step(some_rounds):
+        next(some_rounds, None)
+
+    def load(src, dst, at):
+        copy = pltpu.make_async_copy(src, dst, load_sems.at[at])
+        copy.start()
+        return copy
+
+    load_message = [load(audio_hbm, audio_ref, 3), load(send_hbm, send_ref, 4)]
+    load_small = [
+        load(src, dst, 5 + at)
+        for at, (src, dst) in enumerate(
+            (
+                (place_hbm, place_ref),
+                (wz_hbm, wz_ref),
+                (gz_hbm, gz_ref),
+                (bz_hbm, bz_ref),
+                (g1_hbm, g1_ref),
+                (b1_hbm, b1_ref),
+            )
+        )
+    ]
+    load_w = load(w_hbm, w_ref, 0)
+    load_cot = load(cot_hbm, cot_ref, 1)
 
     spread_lanes = one_hot(
         jnp.bitwise_and(iota((40, lanes), 1), group - 1) == iota((40, lanes), 0)
     )
+    for copy in load_message:
+        copy.wait()
     blocks = dot(audio_ref[...], spread_lanes, TN).astype(BF16)
     chosen = one_hot(iota((n_rows, n_dp * slots), 0) == send_ref[...])
     picked = dot(chosen, blocks, TN)
@@ -209,7 +256,9 @@
     for d in range(n_dp):
         msg[d // n_y, d % n_y] = message[d : d + 1]
 
-    pl.semaphore_wait(barrier, n_near - 1 + n_y - 1 + n_z - 1)
+    pl.semaphore_wait(barrier, n_near - 1 + len(y_next) + len(z_next))
+    step(y_rounds)
+    step(z_rounds)
 
     def near_copy(k):
         at, device = near_peer(k)
@@ -226,6 +275,8 @@
         near_copy(k).start()
     got_msg[near] = msg[near]
 
+    for copy in load_small:
+        copy.wait()
     wz_pad[...] = jnp.zeros_like(wz_pad)
     wz_pad[0:10, :] = wz_ref[...]
     gain_zero, bias_zero = gz_ref[...], bz_ref[...]
@@ -234,6 +285,7 @@
     placed = one_hot(iota((n_dp * slots, n_rows), 0) == place_ref[...])
     slot_near, slot_y = of_slot((n_dp * slots, n_dp), 0)
     spread_slots = one_hot(slot_y * n_near + slot_near == iota((n_dp * slots, n_dp), 1))
+    step(y_rounds)
     lane_in, lane_out = iota((lanes, lanes), 0), iota((lanes, lanes), 1)
     sample_in = jnp.bitwise_and(lane_in, group - 1)
     sample_out = jnp.bitwise_and(lane_out, group - 1)
@@ -243,6 +295,7 @@
     widen = one_hot(lax.shift_right_logical(row_id, 2) == iota((n_out, n_rows), 1))
     phase = jnp.bitwise_and(iota((n_out, lanes), 0), 3)
     own_phase = phase == lax.shift_right_logical(iota((n_out, lanes), 1), 6)
+    step(y_rounds)
     tap = sample_in - 10 * lax.shift_right_logical(lane_in, 6)
     wanted = jnp.where(lane_out < 128, lane_out, lane_out - 128 + 5)
     limit = jnp.where(lane_out < 128, 10, 15)
@@ -251,6 +304,8 @@
     edge_limit = jnp.where(lane_out < 128, 10, 5)
     to_edge = one_hot((sample_in == edge_from) & (edge_from < edge_limit))
 
+    for _ in range(n_y):
+        step(y_rounds)
     for k in range(1, n_near):
         near_copy(k).wait_recv()
 
@@ -298,6 +353,7 @@
     rows = jnp.where(own_phase, rows, 0.0).astype(BF16)
     patches[0:n_out, :] = dot(rows, to_patch).astype(BF16)
 
+    step(z_rounds)
     def forward_even(r, n):
         pre = dot(patches[pl.ds(r, n), 0:128], wz_pad[...])
         act, scaled, spread, slope = norm_gelu(pre, gain_zero, bias_zero)
@@ -322,6 +378,7 @@
 
     lax.fori_loop(0, n_out // chunk_zero, forward_zero, 0)
 
+    step(z_rounds)
     rim_copy.wait_recv()
     edge = rim[0:1, :] * keep
     tail_id = iota((tail_rows, 128), 0)
@@ -335,6 +392,7 @@
     act_even[n_out:n_even, :] = (forward_even(n_out, tail_rows) * keep).astype(BF16)
     load_w.wait()
 
+    step(z_rounds)
     third[...] = dot(act_even[...], w_ref[2 * width : 3 * width, :])
     for r in range(0, n_out, 64):
         third[r : r + 64, :] = third[r + 1 : r + 65, :]
@@ -365,6 +423,7 @@
     sum_gain_one, sum_bias_one = lax.fori_loop(
         0, n_out // chunk_one, layer_one, (zero_sum, zero_sum)
     )
+    step(z_rounds)
     back_down[...] = back_f32[7 : 7 + n_even, :].astype(BF16)
 
     keep_feats = pltpu.make_async_copy(feats_ref, feats_hbm, load_sems.at[2])
@@ -589,6 +648,8 @@
         for j in range(per_owner):
             grad_ref[8 * j : 8 * j + 8, q * cols : (q + 1) * cols] = total[j]
 
+    for _ in range(n_z):
+        step(z_rounds)
     along_y(1)
     small_core_copy.wait_recv()
     small_z[z] = (small[core] + small_core[...]).astype(BF16)
@@ -673,6 +734,11 @@
     page = lambda *shape: pltpu.VMEM((*shape, per_owner, 8, width // quarters), BF16)
     dma = lambda *shape: pltpu.SemaphoreType.DMA(shape)
     scratch = [
+        vmem(40, n_rows, dtype=BF16),
+        vmem(1, n_dp * slots, dtype=jnp.int32),
+        vmem(1, n_rows, dtype=jnp.int32),
+        vmem(10, width, dtype=BF16),
+        *[vmem(1, width)] * 4,
         vmem(n_out, width, dtype=BF16),
         vmem(3 * width, width, dtype=BF16),
         vmem(n_out, width, dtype=BF16),
@@ -716,7 +782,7 @@
         vmem(n_y, 8, width),
         vmem(n_z, 8, width, dtype=BF16),
         vmem(8, width),
-        dma(3),
+        dma(11),
         dma(n_near),
         dma(n_near),
         dma(n_y),
@@ -738,6 +804,8 @@
         dma(n_z),
         dma(n_z),
         dma(2),
+        pltpu.SemaphoreType.REGULAR((2,)),
+        pltpu.SemaphoreType.REGULAR((2,)),
     ]
     row = jax.ShapeDtypeStruct((1, width), F32)
     in_vmem = pl.BlockSpec(memory_space=pltpu.VMEM)
@@ -749,7 +817,7 @@
             jax.ShapeDtypeStruct((3 * width // n_dp, width), F32),
             jax.ShapeDtypeStruct((2, 8, width), F32),
         ),
-        in_specs=[in_vmem, in_vmem, in_vmem, anywhere, in_vmem, anywhere, *[in_vmem] * 4],
+        in_specs=[anywhere] * 10,
         out_specs=(anywhere, in_vmem, in_vmem),
         scratch_shapes=scratch,
         compiler_params=pltpu.CompilerParams(

time: 66.9 us -> 66.1 us (0.988)
  Pallas kernels: 66 us -> 65.3 us
    pallas_call x1, Pallas kernels: 64.1 us -> 63.4 us  [on_device(): pl.pallas_call(functools.partial(kernel, (n_dp, n_x, n_z, n_rows, n_out,...]
where the time goes in v4:
time: 66.1 us; the launch traced here: 65.9 us
  Pallas kernels  65.3 us (99%)
    pallas_call x1, Pallas kernels, on_device(): pl.pallas_call(functools.partial(kernel, (n_dp, n_x, n_z, n_rows, n_out,...  63.4 us
    pallas_call x1, Pallas kernels, on_device(): pl.pallas_call(hand_out, out_shape=(jax.ShapeDtypeStruct(feats.shape, fea...  1.91 us

profile of v4, /device:TPU:1, one launch (start us, length us, event | category | flops | bytes accessed | tf_op | source)
XLA Modules:
  0.0 65.9 jit_solution(13114544928829086183)
XLA Ops:
  0.6 63.4 %shard_map.153 = (bf16[512,512]{1,0:T(8,128)(2,1)}, f32[24,512]{1,0:T(8,128)}, f32[2,8,512]{2,1,0:T(8,128)}) custom-call(bf16[40,128]{1,0:T(8,128)(2,1)} %bitcast.16, s32[1,256]{1,0:T(1,128)} %bitcast.21, s32[1,128]{1,0:T(1,128)} %bitcast.22, bf16[512,512]{1,0:T(8,128)(2,1)} %bitcast.15, bf16[10,512]{1,0:T(8,128)(2,1)} %wz_hbm.1, bf16[1536,512]{1,0:T(8,128)(2,1)} %w_hbm.1, ...), custom_call_target="tpu_custom_call" | custom-call | tf_op jit(solution)/shard_map/pallas_call | solution.py:813
  64.0 1.9 %shard_map.154 = (bf16[512,512]{1,0:T(8,128)(2,1)}, f32[24,512]{1,0:T(8,128)}, f32[10,512]{1,0:T(8,128)}, f32[1,512]{1,0:T(1,128)}, f32[1,512]{1,0:T(1,128)}, /*index=5*/f32[1,512]{1,0:T(1,128)}, f32[1,512]{1,0:T(1,128)}) custom-call(bf16[512,512]{1,0:T(8,128)(2,1)} %get-tuple-element.17.feats_in, f32[24,512]{1,0:T(8,128)} %get-tuple-element.18.grad_in, ...), custom_call_target="tpu_custom_call" | custom-call | tf_op jit(solution)/shard_map/pallas_call | solution.py:838

commit v5 on v4

--- a/solution.py
+++ b/solution.py
@@ -16,9 +16,9 @@
 slots = 4
 group = 64
 lanes = slots * group
-chunk_zero = 128
-chunk_one = 128
-chunk_back = 128
+chunk_zero = 512
+chunk_one = 512
+chunk_back = 256
 tail_rows = 16
 quarters = 4
 

time: 66.1 us -> 63.7 us (0.964)
  Pallas kernels: 65.3 us -> 62.9 us
    pallas_call x1, Pallas kernels: 63.4 us -> 61 us  [on_device(): pl.pallas_call(functools.partial(kernel, (n_dp, n_x, n_z, n_rows, n_out,...]
where the time goes in v5:
time: 63.7 us; the launch traced here: 63.6 us
  Pallas kernels  62.9 us (99%)
  between operations  0.64 us (1%)
    pallas_call x1, Pallas kernels, on_device(): pl.pallas_call(functools.partial(kernel, (n_dp, n_x, n_z, n_rows, n_out,...  61 us
    pallas_call x1, Pallas kernels, on_device(): pl.pallas_call(hand_out, out_shape=(jax.ShapeDtypeStruct(feats.shape, fea...  1.91 us

profile of v5, /device:TPU:1, one launch (start us, length us, event | category | flops | bytes accessed | tf_op | source)
XLA Modules:
  0.0 63.6 jit_solution(7470843207998627623)
XLA Ops:
  0.6 61.0 %shard_map.153 = (bf16[512,512]{1,0:T(8,128)(2,1)}, f32[24,512]{1,0:T(8,128)}, f32[2,8,512]{2,1,0:T(8,128)}) custom-call(bf16[40,128]{1,0:T(8,128)(2,1)} %bitcast.16, s32[1,256]{1,0:T(1,128)} %bitcast.21, s32[1,128]{1,0:T(1,128)} %bitcast.22, bf16[512,512]{1,0:T(8,128)(2,1)} %bitcast.15, bf16[10,512]{1,0:T(8,128)(2,1)} %wz_hbm.1, bf16[1536,512]{1,0:T(8,128)(2,1)} %w_hbm.1, ...), custom_call_target="tpu_custom_call" | custom-call | tf_op jit(solution)/shard_map/pallas_call | solution.py:813
  61.7 1.9 %shard_map.154 = (bf16[512,512]{1,0:T(8,128)(2,1)}, f32[24,512]{1,0:T(8,128)}, f32[10,512]{1,0:T(8,128)}, f32[1,512]{1,0:T(1,128)}, f32[1,512]{1,0:T(1,128)}, /*index=5*/f32[1,512]{1,0:T(1,128)}, f32[1,512]{1,0:T(1,128)}) custom-call(bf16[512,512]{1,0:T(8,128)(2,1)} %get-tuple-element.17.feats_in, f32[24,512]{1,0:T(8,128)} %get-tuple-element.18.grad_in, ...), custom_call_target="tpu_custom_call" | custom-call | tf_op jit(solution)/shard_map/pallas_call | solution.py:838

commit v6 on v5

--- a/solution.py
+++ b/solution.py
@@ -285,7 +285,27 @@
     placed = one_hot(iota((n_dp * slots, n_rows), 0) == place_ref[...])
     slot_near, slot_y = of_slot((n_dp * slots, n_dp), 0)
     spread_slots = one_hot(slot_y * n_near + slot_near == iota((n_dp * slots, n_dp), 1))
-    step(y_rounds)
+    for _ in range(n_y):
+        step(y_rounds)
+    for k in range(1, n_near):
+        near_copy(k).wait_recv()
+
+    def far_copy(k):
+        at, device = y_peer(k)
+        return pltpu.make_async_remote_copy(
+            src_ref=got_msg.at[:, at],
+            dst_ref=arr.at[y],
+            send_sem=far_send.at[k],
+            recv_sem=far_recv.at[k],
+            device_id={"dp": device},
+            device_id_type=MESH,
+        )
+
+    order_y = sorted(range(1, n_y), key=lambda k: -min(k, n_y - k))
+    order_z = sorted(range(1, n_z), key=lambda k: -min(k, n_z - k))
+    for k in order_y:
+        far_copy(k).start()
+    arr[y] = got_msg[:, y]
     lane_in, lane_out = iota((lanes, lanes), 0), iota((lanes, lanes), 1)
     sample_in = jnp.bitwise_and(lane_in, group - 1)
     sample_out = jnp.bitwise_and(lane_out, group - 1)
@@ -295,7 +315,6 @@
     widen = one_hot(lax.shift_right_logical(row_id, 2) == iota((n_out, n_rows), 1))
     phase = jnp.bitwise_and(iota((n_out, lanes), 0), 3)
     own_phase = phase == lax.shift_right_logical(iota((n_out, lanes), 1), 6)
-    step(y_rounds)
     tap = sample_in - 10 * lax.shift_right_logical(lane_in, 6)
     wanted = jnp.where(lane_out < 128, lane_out, lane_out - 128 + 5)
     limit = jnp.where(lane_out < 128, 10, 15)
@@ -304,27 +323,6 @@
     edge_limit = jnp.where(lane_out < 128, 10, 5)
     to_edge = one_hot((sample_in == edge_from) & (edge_from < edge_limit))
 
-    for _ in range(n_y):
-        step(y_rounds)
-    for k in range(1, n_near):
-        near_copy(k).wait_recv()
-
-    def far_copy(k):
-        at, device = y_peer(k)
-        return pltpu.make_async_remote_copy(
-            src_ref=got_msg.at[:, at],
-            dst_ref=arr.at[y],
-            send_sem=far_send.at[k],
-            recv_sem=far_recv.at[k],
-            device_id={"dp": device},
-            device_id_type=MESH,
-        )
-
-    order_y = sorted(range(1, n_y), key=lambda k: -min(k, n_y - k))
-    order_z = sorted(range(1, n_z), key=lambda k: -min(k, n_z - k))
-    for k in order_y:
-        far_copy(k).start()
-    arr[y] = got_msg[:, y]
     for k in range(1, n_y):
         far_copy(k).wait_recv()
 

time: 63.7 us -> 63.8 us (level)
  no operation moved by 1% of the time
where the time goes in v6:
time: 63.8 us; the launch traced here: 63.6 us
  Pallas kernels  62.9 us (99%)
  between operations  0.64 us (1%)
    pallas_call x1, Pallas kernels, on_device(): pl.pallas_call(functools.partial(kernel, (n_dp, n_x, n_z, n_rows, n_out,...  61 us
    pallas_call x1, Pallas kernels, on_device(): pl.pallas_call(hand_out, out_shape=(jax.ShapeDtypeStruct(feats.shape, fea...  1.91 us

profile of v6, /device:TPU:1, one launch (start us, length us, event | category | flops | bytes accessed | tf_op | source)
XLA Modules:
  0.0 63.6 jit_solution(15443390104543256677)
XLA Ops:
  0.6 61.0 %shard_map.153 = (bf16[512,512]{1,0:T(8,128)(2,1)}, f32[24,512]{1,0:T(8,128)}, f32[2,8,512]{2,1,0:T(8,128)}) custom-call(bf16[40,128]{1,0:T(8,128)(2,1)} %bitcast.16, s32[1,256]{1,0:T(1,128)} %bitcast.21, s32[1,128]{1,0:T(1,128)} %bitcast.22, bf16[512,512]{1,0:T(8,128)(2,1)} %bitcast.15, bf16[10,512]{1,0:T(8,128)(2,1)} %wz_hbm.1, bf16[1536,512]{1,0:T(8,128)(2,1)} %w_hbm.1, ...), custom_call_target="tpu_custom_call" | custom-call | tf_op jit(solution)/shard_map/pallas_call | solution.py:811
  61.7 1.9 %shard_map.154 = (bf16[512,512]{1,0:T(8,128)(2,1)}, f32[24,512]{1,0:T(8,128)}, f32[10,512]{1,0:T(8,128)}, f32[1,512]{1,0:T(1,128)}, f32[1,512]{1,0:T(1,128)}, /*index=5*/f32[1,512]{1,0:T(1,128)}, f32[1,512]{1,0:T(1,128)}) custom-call(bf16[512,512]{1,0:T(8,128)(2,1)} %get-tuple-element.17.feats_in, f32[24,512]{1,0:T(8,128)} %get-tuple-element.18.grad_in, ...), custom_call_target="tpu_custom_call" | custom-call | tf_op jit(solution)/shard_map/pallas_call | solution.py:836
